TPU v7x, 32 devices: a whole 2x2x4 slice. The times are simulated.
32 devices in a mesh: pipe: 2 (over core), seq: 4 (over z), dp: 4 (over y, x).
Axes of the slice: x: 2, y: 2, z: 4, core: 2. Of those that a mesh axis runs over, the one named last changes fastest.
Arguments:
- inputs: bfloat16 [2, 4, 1024, 2048], P(None, 'dp', 'seq'), may hold values from -6 to 6
- cotangent: bfloat16 [2, 4, 1024, 2048], P(None, 'dp', 'seq'), may hold values from -6 to 6
- lengths: int32 [2, 4], replicated, may hold values from 256 to 1024, as said below
- norm_gain: float32 [2, 2048], P('pipe'), may hold values from 0.5 to 1.5
- w_query: float32 [2, 2048, 2048], P('pipe', None, 'seq'), may hold values from -0.125 to 0.125
- w_forget: float32 [2, 2048, 2048], P('pipe', None, 'seq'), may hold values from -0.125 to 0.125
- w_input: float32 [2, 2048, 2048], P('pipe', None, 'seq'), may hold values from -0.125 to 0.125
- lower_bound: float32 [2, 2048], P('pipe', 'seq'), may hold values from 0.4 to 0.9998
- out_gain: float32 [2, 2048], P('pipe', 'seq'), may hold values from 0.5 to 1.5
- w_output: float32 [2, 2048, 2048], P('pipe', 'seq'), may hold values from -0.125 to 0.125
- ffn_gain: float32 [2, 2048], P('pipe'), may hold values from 0.5 to 1.5
- w_gate: float32 [2, 2048, 5632], P('pipe', None, 'seq'), may hold values from -0.125 to 0.125
- w_up: float32 [2, 2048, 5632], P('pipe', None, 'seq'), may hold values from -0.125 to 0.125
- w_down: float32 [2, 5632, 2048], P('pipe', 'seq'), may hold values from -0.078125 to 0.078125
Outputs:
- section_outputs: bfloat16 [2, 2, 4, 1024, 2048], P('pipe', None, 'dp', 'seq')
- input_grads: float32 [2, 2, 4, 1024, 2048], P('pipe', None, 'dp', 'seq')
- grad_norm_gain: float32 [2, 2048], P('pipe')
- grad_query: float32 [2, 2048, 2048], P('pipe', None, 'seq')
- grad_forget: float32 [2, 2048, 2048], P('pipe', None, 'seq')
- grad_input: float32 [2, 2048, 2048], P('pipe', None, 'seq')
- grad_lower_bound: float32 [2, 2048], P('pipe', 'seq')
- grad_out_gain: float32 [2, 2048], P('pipe', 'seq')
- grad_output: float32 [2, 2048, 2048], P('pipe', 'seq')
- grad_ffn_gain: float32 [2, 2048], P('pipe')
- grad_gate: float32 [2, 2048, 5632], P('pipe', None, 'seq')
- grad_up: float32 [2, 2048, 5632], P('pipe', None, 'seq')
- grad_down: float32 [2, 5632, 2048], P('pipe', 'seq')
Inputs may be any that keep to these rules, and one draw needn't show every extreme that they name: `lengths`: each micro-batch holds one sequence in each row, its valid tokens at the start of the row; some row is full (1024) and some has exactly 256.
All inputs are finite; a program needn't handle non-finite values.
Results may differ from a plain program's by a relative error of at most 0.035.
Values may be sent and summed in bfloat16 or wider, within the bound.
A program may use at most 576 MiB of HBM per device.

v0:
```python
import jax
import jax.numpy as jnp
from jax import lax
from jax.sharding import PartitionSpec as P

D = 2048
HEADS = 16
SPAN = 64
BLOCK = 512


EPSILON = 1e-06


def shortened(array):
    return jax.tree.map(lambda a: a.astype(jnp.bfloat16) if a.dtype == jnp.float32 else a, array)


def shifted(block, axis, distance):
    devices = range(lax.axis_size(axis))
    route = [(i - distance, i) for i in devices if i - distance in devices]
    return lax.ppermute(block, axis, route)


def rms_norm(values_in, gain):
    return (
        values_in
        * lax.rsqrt(jnp.mean(values_in * values_in, axis=-1, keepdims=True) + EPSILON)
        * gain
    )


def gate_terms(forget_raw, bound):
    forget_log = jnp.log(bound + (1.0 - bound) * jax.nn.sigmoid(forget_raw))
    keys_in = (1.0 - bound) * jax.nn.sigmoid(-forget_raw)
    return (forget_log, keys_in)


def intra_part(parts):
    query_blocks, key_blocks, value_blocks, cumul = parts
    differ = cumul[:, :, None] - cumul[:, None, :]
    lower = (jnp.arange(SPAN)[:, None] >= jnp.arange(SPAN)[None, :]).astype(jnp.float32)
    weight = jnp.exp(jnp.minimum(differ, 0.0)) * lower[None, :, :, None, None]
    scores = jnp.sum(weight * query_blocks[:, :, None] * key_blocks[:, None, :], axis=-1)
    return jnp.einsum("ntsh,nshe->nthe", scores, value_blocks, precision=lax.Precision.HIGHEST)


def recurrence(queries, forget_log, keys_in, values_in):
    length, heads_count, head_dim = queries.shape
    spans = length // SPAN
    shape_four = (spans, SPAN, heads_count, head_dim)
    query_blocks = queries.reshape(shape_four)
    key_blocks = keys_in.reshape(shape_four)
    value_blocks = values_in.reshape(shape_four)
    cumul = jnp.cumsum(forget_log.reshape(shape_four), axis=1)
    ending = cumul[:, -1]
    weighted_keys = key_blocks * jnp.exp(ending[:, None] - cumul)
    updates = jnp.einsum(
        "nchd,nche->nhde", weighted_keys, value_blocks, precision=lax.Precision.HIGHEST
    )
    decays = jnp.exp(ending)

    def advance(state, pair):
        update, decay = pair
        return (decay[..., None] * state + update, state)

    start_state = jnp.zeros((heads_count, head_dim, head_dim), jnp.float32)
    _, before = lax.scan(advance, start_state, (updates, decays))
    carried = jnp.einsum(
        "nchd,nhde->nche", query_blocks * jnp.exp(cumul), before, precision=lax.Precision.HIGHEST
    )
    per_group = BLOCK // SPAN
    groups = spans // per_group

    def regroup(array_in):
        return array_in.reshape((groups, per_group) + array_in.shape[1:])

    within = lax.map(
        jax.checkpoint(intra_part),
        (regroup(query_blocks), regroup(key_blocks), regroup(value_blocks), regroup(cumul)),
    )
    result = carried + within.reshape(shape_four)
    return result.reshape(length, heads_count, head_dim)


def sum_grads(weight_grads):
    return jax.tree.map(
        lambda part: part.astype(jnp.float32), lax.psum(shortened(weight_grads), "dp")
    )


def body(
    inputs,
    cotangent,
    lengths,
    norm_gain,
    w_query,
    w_forget,
    w_input,
    lower_bound,
    out_gain,
    w_output,
    ffn_gain,
    w_gate,
    w_up,
    w_down,
):
    micro_count = inputs.shape[0]
    local_rows = inputs.shape[2]
    width = inputs.shape[3]
    slot_count = local_rows * lax.axis_size("seq")
    head_dim = D // HEADS
    first_section = lax.axis_index("pipe") == 0
    seq_row = lax.axis_index("dp")
    own_lengths = lax.dynamic_index_in_dim(lengths, seq_row, axis=1, keepdims=False)
    positions = lax.axis_index("seq") * local_rows + jnp.arange(local_rows, dtype=jnp.int32)
    token_masks = (positions[None, :] < own_lengths[:, None]).astype(jnp.float32)
    gain_one = norm_gain[0]
    gain_two = ffn_gain[0]
    bound = lower_bound[0]
    head_gain = out_gain[0]
    local_width = w_query.shape[2]
    heads_here = local_width // head_dim
    hidden_here = w_gate.shape[2]
    w_proj = jnp.concatenate([w_query[0], w_forget[0], w_input[0]], axis=1).astype(jnp.bfloat16)
    w_out = w_output[0].astype(jnp.bfloat16)
    w_pair = jnp.concatenate([w_gate[0], w_up[0]], axis=1).astype(jnp.bfloat16)
    w_down_local = w_down[0].astype(jnp.bfloat16)

    def mixer_core(projected, bound_in):
        queries = projected[:, :local_width]
        forget_raw = projected[:, local_width : 2 * local_width]
        values_in = projected[:, 2 * local_width :]
        forget_log, keys_in = gate_terms(forget_raw, bound_in)
        shape_three = (slot_count, heads_here, head_dim)
        mixed = recurrence(
            queries.reshape(shape_three),
            forget_log.reshape(shape_three),
            keys_in.reshape(shape_three),
            values_in.reshape(shape_three),
        )
        return mixed.reshape(slot_count, local_width)

    def mixer_front(residual):
        normed = rms_norm(residual, gain_one).astype(jnp.bfloat16)
        normed_all = lax.all_gather(normed, "seq", axis=0, tiled=True)
        projected = jnp.dot(normed_all, w_proj, preferred_element_type=jnp.float32)
        mixed = mixer_core(projected, bound)
        squares = lax.psum(jnp.sum(mixed * mixed, axis=1), "seq")
        inv_rms = lax.rsqrt(squares / D + EPSILON)
        head_normed = (mixed * inv_rms[:, None] * head_gain).astype(jnp.bfloat16)
        return (normed_all, projected, mixed, inv_rms, head_normed)

    def ffn_front(middle):
        normed_two = rms_norm(middle, gain_two).astype(jnp.bfloat16)
        normed_two_all = lax.all_gather(normed_two, "seq", axis=0, tiled=True)
        paired = jnp.dot(normed_two_all, w_pair, preferred_element_type=jnp.float32)
        gate_act = paired[:, :hidden_here]
        up_act = paired[:, hidden_here:]
        hidden = (jax.nn.silu(gate_act) * up_act).astype(jnp.bfloat16)
        return (normed_two_all, gate_act, up_act, hidden)

    def backward_block(block_in, token_mask, middle, grad_out):
        residual = block_in.astype(jnp.float32)
        normed_all, projected, mixed, inv_rms, head_normed = mixer_front(residual)
        normed_two_all, gate_act, up_act, hidden = ffn_front(middle)
        masked = token_mask[:, None] * grad_out
        grad_branch = masked.astype(jnp.bfloat16)
        grad_branch_all = lax.all_gather(grad_branch, "seq", axis=0, tiled=True)
        grad_down = jnp.einsum(
            "tf,td->fd", hidden, grad_branch_all, preferred_element_type=jnp.float32
        )
        grad_hidden = jnp.einsum(
            "td,fd->tf", grad_branch_all, w_down_local, preferred_element_type=jnp.float32
        )
        _, pull_gate = jax.vjp(
            lambda gate_in, up_in: jax.nn.silu(gate_in) * up_in, gate_act, up_act
        )
        grad_gate, grad_up = pull_gate(grad_hidden)
        grad_pair = jnp.concatenate([grad_gate, grad_up], axis=1).astype(jnp.bfloat16)
        grad_pair_weight = jnp.einsum(
            "td,tf->df", normed_two_all, grad_pair, preferred_element_type=jnp.float32
        )
        grad_normed_two = lax.psum_scatter(
            jnp.einsum("tf,df->td", grad_pair, w_pair, preferred_element_type=jnp.float32).astype(
                jnp.bfloat16
            ),
            "seq",
            scatter_dimension=0,
            tiled=True,
        ).astype(jnp.float32)
        _, pull_norm = jax.vjp(rms_norm, middle, gain_two)
        grad_middle_norm, grad_gain_two = pull_norm(grad_normed_two)
        grad_middle = masked + grad_middle_norm
        grad_mix = grad_middle.astype(jnp.bfloat16)
        grad_mix_all = lax.all_gather(grad_mix, "seq", axis=0, tiled=True)
        grad_out_weight = jnp.einsum(
            "th,td->hd", head_normed, grad_mix_all, preferred_element_type=jnp.float32
        )
        grad_head = jnp.einsum("td,hd->th", grad_mix_all, w_out, preferred_element_type=jnp.float32)
        scaled = mixed * inv_rms[:, None]
        grad_head_gain = jnp.sum(grad_head * scaled, axis=0)
        inner_sum = lax.psum(jnp.sum(grad_head * head_gain * mixed, axis=1), "seq")
        grad_mixed = (
            grad_head * head_gain * inv_rms[:, None]
            - mixed * (inv_rms * inv_rms * inv_rms * inner_sum / D)[:, None]
        )
        _, pull_core = jax.vjp(mixer_core, projected, bound)
        grad_projected, grad_bound = pull_core(grad_mixed)
        grad_proj_low = grad_projected.astype(jnp.bfloat16)
        grad_proj_weight = jnp.einsum(
            "td,tf->df", normed_all, grad_proj_low, preferred_element_type=jnp.float32
        )
        grad_normed = lax.psum_scatter(
            jnp.einsum(
                "tf,df->td", grad_proj_low, w_proj, preferred_element_type=jnp.float32
            ).astype(jnp.bfloat16),
            "seq",
            scatter_dimension=0,
            tiled=True,
        ).astype(jnp.float32)
        _, pull_first = jax.vjp(rms_norm, residual, gain_one)
        grad_residual_norm, grad_gain_one = pull_first(grad_normed)
        grad_in = grad_middle + grad_residual_norm
        weight_grads = (
            grad_proj_weight,
            grad_bound,
            grad_head_gain,
            grad_out_weight,
            grad_pair_weight,
            grad_down,
        )
        gain_grads = (grad_gain_one, grad_gain_two)
        return (grad_in, weight_grads, gain_grads)

    empty_rows = jnp.zeros((local_rows, width), jnp.bfloat16)
    received = empty_rows
    section_outs = []
    block_ins = []
    middles = []
    masks_used = []
    saves = []
    for moment in range(micro_count + 1):
        source = inputs[moment, 0] if moment < micro_count else empty_rows
        block_in = jnp.where(first_section, source, received)
        token_mask = jnp.where(
            first_section,
            token_masks[min(moment, micro_count - 1)],
            token_masks[max(moment - 1, 0)],
        )
        forward_residual = block_in.astype(jnp.float32)
        front = mixer_front(forward_residual)
        forward_head_normed = front[4]
        branch = lax.psum_scatter(
            jnp.dot(forward_head_normed, w_out, preferred_element_type=jnp.float32).astype(
                jnp.bfloat16
            ),
            "seq",
            scatter_dimension=0,
            tiled=True,
        ).astype(jnp.float32)
        forward_middle = forward_residual + branch
        back_part = ffn_front(forward_middle)
        forward_hidden = back_part[3]
        ffn_branch = lax.psum_scatter(
            jnp.dot(forward_hidden, w_down_local, preferred_element_type=jnp.float32).astype(
                jnp.bfloat16
            ),
            "seq",
            scatter_dimension=0,
            tiled=True,
        ).astype(jnp.float32)
        block_out = token_mask[:, None] * (forward_middle + ffn_branch)
        block_out, middle, saved = (block_out, forward_middle, front + back_part)
        out_low = block_out.astype(jnp.bfloat16)
        section_outs.append(out_low)
        block_ins.append(block_in)
        middles.append(middle)
        masks_used.append(token_mask)
        saves.append(saved)
        if moment < micro_count:
            received = shifted(out_low, "pipe", 1)

    def select_pair(early, late):
        return jax.tree.map(
            lambda early_item, late_item: jnp.where(first_section, early_item, late_item),
            early,
            late,
        )

    received_back = empty_rows
    grad_ins = []
    weight_total = None
    gain_total = None
    for moment in range(micro_count + 1):
        low_index = max(moment - 1, 0)
        high_index = min(moment + 1, micro_count)
        block_in = select_pair(block_ins[low_index], block_ins[high_index])
        token_mask = select_pair(masks_used[low_index], masks_used[high_index])
        middle = select_pair(middles[low_index], middles[high_index])
        saved = select_pair(saves[low_index], saves[high_index])
        source_grad = (
            cotangent[moment, 0].astype(jnp.float32)
            if moment < micro_count
            else jnp.zeros((local_rows, width), jnp.float32)
        )
        grad_out = jnp.where(first_section, received_back.astype(jnp.float32), source_grad)
        grad_in, weight_grads, gain_grads = backward_block(block_in, token_mask, middle, grad_out)
        if weight_total is None:
            weight_total = weight_grads
            gain_total = gain_grads
        else:
            weight_total = jax.tree.map(
                lambda left, right: left + right, weight_total, weight_grads
            )
            gain_total = jax.tree.map(lambda left, right: left + right, gain_total, gain_grads)
        grad_ins.append(grad_in)
        if moment < micro_count:
            received_back = shifted(grad_in.astype(jnp.bfloat16), "pipe", -1)
    summed = sum_grads(weight_total)
    gains_summed = lax.psum(gain_total, ("seq", "dp"))
    grad_proj_weight, grad_bound, grad_head_gain, grad_out_weight, grad_pair_weight, grad_down = (
        summed
    )
    section_outputs = jnp.stack(
        [
            jnp.where(first_section, section_outs[mb_index], section_outs[mb_index + 1])
            for mb_index in range(micro_count)
        ]
    )[None, :, None]
    input_grads = jnp.stack(
        [
            jnp.where(first_section, grad_ins[mb_index + 1], grad_ins[mb_index])
            for mb_index in range(micro_count)
        ]
    )[None, :, None]
    grad_query = grad_proj_weight[:, :local_width][None]
    grad_forget = grad_proj_weight[:, local_width : 2 * local_width][None]
    grad_input = grad_proj_weight[:, 2 * local_width :][None]
    grad_gate = grad_pair_weight[:, :hidden_here][None]
    grad_up = grad_pair_weight[:, hidden_here:][None]
    return (
        section_outputs,
        input_grads,
        gains_summed[0][None],
        grad_query,
        grad_forget,
        grad_input,
        grad_bound[None],
        grad_head_gain[None],
        grad_out_weight[None],
        gains_summed[1][None],
        grad_gate,
        grad_up,
        grad_down[None],
    )


def solution(mesh):
    in_specs = (
        P(None, "dp", "seq", None),
        P(None, "dp", "seq", None),
        P(),
        P("pipe", None),
        P("pipe", None, "seq"),
        P("pipe", None, "seq"),
        P("pipe", None, "seq"),
        P("pipe", "seq"),
        P("pipe", "seq"),
        P("pipe", "seq", None),
        P("pipe", None),
        P("pipe", None, "seq"),
        P("pipe", None, "seq"),
        P("pipe", "seq", None),
    )
    out_specs = (
        P("pipe", None, "dp", "seq", None),
        P("pipe", None, "dp", "seq", None),
        P("pipe", None),
        P("pipe", None, "seq"),
        P("pipe", None, "seq"),
        P("pipe", None, "seq"),
        P("pipe", "seq"),
        P("pipe", "seq"),
        P("pipe", "seq", None),
        P("pipe", None),
        P("pipe", None, "seq"),
        P("pipe", None, "seq"),
        P("pipe", "seq", None),
    )
    return jax.shard_map(body, mesh=mesh, in_specs=in_specs, out_specs=out_specs, check_vma=False)
```

profile of v0, /device:TPU:0, one launch (start us, length us, event | category | flops | bytes accessed | tf_op | source)
XLA Modules:
  0.0 4576.6 jit_solution(7347395333932327453)
XLA Ops:
  21.7 73.4 %all-gather.19.cloned.1.call-done = bf16[1024,2048]{1,0:T(8,128)(2,1)} async-done(((bf16[256,2048]{1,0:T(8,128)(2,1)}), bf16[1024,2048]{1,0:T(8,128)(2,1)}) %all-gather.19.cloned.1.call-update) | async-done | bytes 4194320 | tf_op jit(solution)/shard_map/all_gather | solution.py:146
  129.6 71.1 %while.300 = (s32[]{:T(128)}, f32[2,8,64,4,128]{4,2,3,1,0:T(8,128)}, f32[2,8,64,4,128]{4,3,2,1,0:T(4,128)}, f32[2,8,64,4,128]{4,1,0,2,3:T(8,128)S(1)}, f32[2,8,6...) while((s32[]{:T(128)}, f32[2,8,64,4,128]{4,2,3,1,0:T(8,128)}, ...), condition=%wide.region_6.7_spmd, body=%wide.region_4.6_spmd.sunk | while | flops 301867008 | bytes 33063044 | solution.py:78
  137.5 24.5 multiply_reduce_fusion.30
  173.0 24.5 multiply_reduce_fusion.30
  218.2 30.4 while.309
  271.7 75.9 %reduce-scatter.13.cloned.1.call-done = bf16[256,2048]{1,0:T(8,128)(2,1)} async-done(((bf16[1024,2048]{1,0:T(8,128)(2,1)}), bf16[256,2048]{1,0:T(8,128)(2,1)}) %reduce-scatter.13.cloned.1.call-update) | async-done | bytes 1048592 | tf_op jit(solution)/shard_map/reduce_scatter | solution.py:254
  372.3 60.0 %all-gather.21.cloned.1.call-done = bf16[1024,2048]{1,0:T(8,128)(2,1)} async-done(((bf16[256,2048]{1,0:T(8,128)(2,1)}), bf16[1024,2048]{1,0:T(8,128)(2,1)}) %all-gather.21.cloned.1.call-update) | async-done | bytes 4194320 | tf_op jit(solution)/shard_map/all_gather | solution.py:156
  465.7 74.5 %reduce-scatter.15.cloned.1.call-done = bf16[256,2048]{1,0:T(8,128)(2,1)} async-done(((bf16[1024,2048]{1,0:T(8,128)(2,1)}), bf16[256,2048]{1,0:T(8,128)(2,1)}) %reduce-scatter.15.cloned.1.call-update) | async-done | bytes 1048592 | tf_op jit(solution)/shard_map/reduce_scatter | solution.py:265
  549.7 81.0 %all-gather.23.cloned.1.call-done = bf16[1024,2048]{1,0:T(8,128)(2,1)} async-done(((bf16[256,2048]{1,0:T(8,128)(2,1)}), bf16[1024,2048]{1,0:T(8,128)(2,1)}) %all-gather.23.cloned.1.call-update) | async-done | bytes 4194320 | tf_op jit(solution)/shard_map/all_gather | solution.py:146
  642.3 69.7 %all-gather.35.cloned.1.call-done = bf16[1024,2048]{1,0:T(8,128)(2,1)} async-done(((bf16[256,2048]{1,0:T(8,128)(2,1)}), bf16[1024,2048]{1,0:T(8,128)(2,1)}) %all-gather.35.cloned.1.call-update) | async-done | bytes 4194320 | tf_op jit(solution)/shard_map/all_gather | solution.py:146
  775.6 70.9 %while.301 = (s32[]{:T(128)}, f32[2,8,64,4,128]{4,2,3,1,0:T(8,128)}, f32[2,8,64,4,128]{4,3,2,1,0:T(4,128)}, f32[2,8,64,4,128]{4,1,0,2,3:T(8,128)}, f32[2,8,64,4,...) while((s32[]{:T(128)}, f32[2,8,64,4,128]{4,2,3,1,0:T(8,128)}, ...), condition=%wide.region_18.19_spmd, body=%wide.region_16.18_spmd.sunk | while | flops 301867008 | bytes 41451680 | solution.py:78
  783.3 24.5 multiply_reduce_fusion.31
  818.7 24.5 multiply_reduce_fusion.31
  864.7 30.0 while.310
  912.3 66.9 %while.303 = (s32[]{:T(128)}, f32[2,8,64,4,128]{4,2,3,1,0:T(8,128)}, f32[2,8,64,4,128]{4,2,3,1,0:T(8,128)}, f32[2,8,64,4,128]{4,2,3,1,0:T(8,128)}, f32[2,8,64,4,...) while((s32[]{:T(128)}, f32[2,8,64,4,128]{4,2,3,1,0:T(8,128)}, ...), condition=%wide.region_45.46_spmd, body=%wide.region_43.45_spmd.sunk | while | flops 301867008 | bytes 24675448 | solution.py:78
  918.1 24.2 multiply_reduce_fusion.33
  951.4 24.2 multiply_reduce_fusion.33
  993.2 40.7 while.312
  1058.9 75.9 %reduce-scatter.17.cloned.1.call-done = bf16[256,2048]{1,0:T(8,128)(2,1)} async-done(((bf16[1024,2048]{1,0:T(8,128)(2,1)}), bf16[256,2048]{1,0:T(8,128)(2,1)}) %reduce-scatter.17.cloned.1.call-update) | async-done | bytes 1048592 | tf_op jit(solution)/shard_map/reduce_scatter | solution.py:254
  1138.2 81.4 %all-gather.25.cloned.1.call-done = bf16[1024,2048]{1,0:T(8,128)(2,1)} async-done(((bf16[256,2048]{1,0:T(8,128)(2,1)}), bf16[1024,2048]{1,0:T(8,128)(2,1)}) %all-gather.25.cloned.1.call-update) | async-done | bytes 4194320 | tf_op jit(solution)/shard_map/all_gather | solution.py:156
  1253.4 74.2 %reduce-scatter.19.cloned.1.call-done = bf16[256,2048]{1,0:T(8,128)(2,1)} async-done(((bf16[1024,2048]{1,0:T(8,128)(2,1)}), bf16[256,2048]{1,0:T(8,128)(2,1)}) %reduce-scatter.19.cloned.1.call-update) | async-done | bytes 1048592 | tf_op jit(solution)/shard_map/reduce_scatter | solution.py:265
  1351.6 60.5 %while.313 = (s32[]{:T(128)}, f32[4,128,128]{2,1,0:T(8,128)S(1)}, f32[16,4,128,128]{3,2,1,0:T(8,128)}, f32[16,4,128,1]{2,1,3,0:T(4,128)}, f32[16,4,128]{2,1,0:T(...) while((s32[]{:T(128)}, f32[4,128,128]{2,1,0:T(8,128)S(1)}, ...), condition=%wide.region_58.59_spmd.clone, body=%wide.region_57.58_spmd.clone.sunk | while | flops 262147 | bytes 1845368 | solution.py:68
  1432.8 68.0 %all-gather.43.cloned.1.call-done = bf16[1024,2048]{1,0:T(8,128)(2,1)} async-done(((bf16[256,2048]{1,0:T(8,128)(2,1)}), bf16[1024,2048]{1,0:T(8,128)(2,1)}) %all-gather.43.cloned.1.call-update) | async-done | bytes 4194320 | tf_op jit(solution)/shard_map/all_gather | solution.py:146
  1555.5 30.0 while.311
  1587.1 71.5 %while.302 = (s32[]{:T(128)}, f32[2,8,64,4,128]{4,2,3,1,0:T(8,128)}, f32[2,8,64,4,128]{4,3,2,1,0:T(4,128)}, f32[2,8,64,4,128]{4,1,0,2,3:T(8,128)S(1)}, f32[2,8,6...) while((s32[]{:T(128)}, f32[2,8,64,4,128]{4,2,3,1,0:T(8,128)}, ...), condition=%wide.region_30.31_spmd, body=%wide.region_28.30_spmd.sunk | while | flops 301867008 | bytes 33063044 | solution.py:78
  1595.2 24.5 multiply_reduce_fusion.32
  1630.8 24.5 multiply_reduce_fusion.32
  1762.1 30.0 while.315
  1792.0 25.3 reduce-scatter.25.cloned.1.call-done
  1826.1 67.2 %while.305 = (s32[]{:T(128)}, f32[2,8,64,4,128]{4,2,3,1,0:T(8,128)}, f32[2,8,64,4,128]{4,2,3,1,0:T(8,128)}, f32[2,8,64,4,128]{4,2,3,1,0:T(8,128)}, f32[2,8,64,4,...) while((s32[]{:T(128)}, f32[2,8,64,4,128]{4,2,3,1,0:T(8,128)}, ...), condition=%wide.region_75.76_spmd, body=%wide.region_73.75_spmd.sunk | while | flops 301867008 | bytes 24675448 | solution.py:78
  1831.9 24.3 multiply_reduce_fusion.34
  1865.4 24.2 multiply_reduce_fusion.34
  1952.2 196.4 %while.304 = (s32[]{:T(128)}, f32[2,8,64,4,128]{4,2,3,1,0:T(8,128)}, f32[2,8,64,4,128]{4,2,3,1,0:T(8,128)}, f32[2,8,64,4,128]{4,2,3,1,0:T(8,128)}, f32[2,8,64,4,...) while((s32[]{:T(128)}, f32[2,8,64,4,128]{4,2,3,1,0:T(8,128)}, ...), condition=%wide.region_56.57_spmd, body=%wide.region_50.56_spmd.sunk | while | flops 754327552 | bytes 107512264 | solution.py:78
  1964.4 77.3 %fusion.506 = (f32[8,64,4,128]{3,1,2,0:T(8,128)}, f32[8,64,4,128]{3,2,1,0:T(4,128)}, f32[8,64,4,128]{3,2,1,0:T(4,128)}, f32[8,64,64,4]{2,3,1,0:T(4,128)}, f32[8,64,4,128]{3,1,2,0:T(8,128)}) fusion(f32[8,64,4,128]{3,2,1,0:T(4,128)} %dynamic-slice_bitcast_fusion.68, f32[8,64,4,128]{3,1,2,0:T(8,128)} %dynamic-slice_bitcast_fusion.69, ...), kind=kLoop, calls=%fused_computation.68.clone.1 | loop fusion | flops 351141888 | bytes 9453568 | tf_op jit(solution)/shard_map/transpose(jvp())/while/body/eval_jaxpr/checkpoint/reduce_sum | solution.py:41
  2062.4 77.3 %fusion.506 = (f32[8,64,4,128]{3,1,2,0:T(8,128)}, f32[8,64,4,128]{3,2,1,0:T(4,128)}, f32[8,64,4,128]{3,2,1,0:T(4,128)}, f32[8,64,64,4]{2,3,1,0:T(4,128)}, f32[8,64,4,128]{3,1,2,0:T(8,128)}) fusion(f32[8,64,4,128]{3,2,1,0:T(4,128)} %dynamic-slice_bitcast_fusion.68, f32[8,64,4,128]{3,1,2,0:T(8,128)} %dynamic-slice_bitcast_fusion.69, ...), kind=kLoop, calls=%fused_computation.68.clone.1 | loop fusion | flops 351141888 | bytes 9453568 | tf_op jit(solution)/shard_map/transpose(jvp())/while/body/eval_jaxpr/checkpoint/reduce_sum | solution.py:41
  2162.6 43.5 while.314
  2264.2 72.4 %reduce-scatter.27.cloned.1.call-done = bf16[256,2048]{1,0:T(8,128)(2,1)} async-done(((bf16[1024,2048]{1,0:T(8,128)(2,1)}), bf16[256,2048]{1,0:T(8,128)(2,1)}) %reduce-scatter.27.cloned.1.call-update) | async-done | bytes 1048592 | tf_op jit(solution)/shard_map/reduce_scatter | solution.py:214
  2354.5 50.9 %while.316 = (s32[]{:T(128)}, f32[4,128,128]{2,1,0:T(8,128)S(1)}, f32[16,4,128,128]{3,2,1,0:T(8,128)}, f32[16,4,128,1]{2,1,3,0:T(4,128)S(1)}, f32[16,4,128]{2,1,...) while((s32[]{:T(128)}, f32[4,128,128]{2,1,0:T(8,128)S(1)}, ...), condition=%wide.region_88.89_spmd.clone, body=%wide.region_87.88_spmd.clone.sunk | while | flops 262147 | bytes 1845368 | solution.py:68
  2479.6 30.3 all-gather.41.cloned.1.call-done
  2529.5 61.0 %all-gather.39.cloned.1.call-done = bf16[1024,2048]{1,0:T(8,128)(2,1)} async-done(((bf16[256,2048]{1,0:T(8,128)(2,1)}), bf16[1024,2048]{1,0:T(8,128)(2,1)}) %all-gather.39.cloned.1.call-update) | async-done | bytes 4194320 | tf_op jit(solution)/shard_map/all_gather | solution.py:169
  2627.5 30.0 while.318
  2657.5 42.8 reduce-scatter.29.cloned.1.call-done
  2709.4 67.1 %while.307 = (s32[]{:T(128)}, f32[2,8,64,4,128]{4,2,3,1,0:T(8,128)}, f32[2,8,64,4,128]{4,2,3,1,0:T(8,128)}, f32[2,8,64,4,128]{4,2,3,1,0:T(8,128)}, f32[2,8,64,4,...) while((s32[]{:T(128)}, f32[2,8,64,4,128]{4,2,3,1,0:T(8,128)}, ...), condition=%wide.region_105.106_spmd, body=%wide.region_103.105_spmd.sunk | while | flops 301867008 | bytes 24675448 | solution.py:78
  2715.2 24.3 multiply_reduce_fusion.35
  2748.7 24.2 multiply_reduce_fusion.35
  2821.1 196.4 %while.306 = (s32[]{:T(128)}, f32[2,8,64,4,128]{4,2,3,1,0:T(8,128)}, f32[2,8,64,4,128]{4,2,3,1,0:T(8,128)}, f32[2,8,64,4,128]{4,2,3,1,0:T(8,128)}, f32[2,8,64,4,...) while((s32[]{:T(128)}, f32[2,8,64,4,128]{4,2,3,1,0:T(8,128)}, ...), condition=%wide.region_86.87_spmd, body=%wide.region_80.86_spmd.sunk | while | flops 754327552 | bytes 107512264 | solution.py:78
  2833.4 77.2 %fusion.517 = (f32[8,64,4,128]{3,1,2,0:T(8,128)}, f32[8,64,4,128]{3,2,1,0:T(4,128)}, f32[8,64,4,128]{3,2,1,0:T(4,128)}, f32[8,64,64,4]{2,3,1,0:T(4,128)}, f32[8,64,4,128]{3,1,2,0:T(8,128)}) fusion(f32[8,64,4,128]{3,2,1,0:T(4,128)} %dynamic-slice_bitcast_fusion.74, f32[8,64,4,128]{3,1,2,0:T(8,128)} %dynamic-slice_bitcast_fusion.75, ...), kind=kLoop, calls=%fused_computation.116.clone.1 | loop fusion | flops 351141888 | bytes 9453568 | tf_op jit(solution)/shard_map/transpose(jvp())/while/body/eval_jaxpr/checkpoint/reduce_sum | solution.py:41
  2931.4 77.2 %fusion.517 = (f32[8,64,4,128]{3,1,2,0:T(8,128)}, f32[8,64,4,128]{3,2,1,0:T(4,128)}, f32[8,64,4,128]{3,2,1,0:T(4,128)}, f32[8,64,64,4]{2,3,1,0:T(4,128)}, f32[8,64,4,128]{3,1,2,0:T(8,128)}) fusion(f32[8,64,4,128]{3,2,1,0:T(4,128)} %dynamic-slice_bitcast_fusion.74, f32[8,64,4,128]{3,1,2,0:T(8,128)} %dynamic-slice_bitcast_fusion.75, ...), kind=kLoop, calls=%fused_computation.116.clone.1 | loop fusion | flops 351141888 | bytes 9453568 | tf_op jit(solution)/shard_map/transpose(jvp())/while/body/eval_jaxpr/checkpoint/reduce_sum | solution.py:41
  3031.5 43.3 while.317
  3130.7 75.0 %reduce-scatter.31.cloned.1.call-done = bf16[256,2048]{1,0:T(8,128)(2,1)} async-done(((bf16[1024,2048]{1,0:T(8,128)(2,1)}), bf16[256,2048]{1,0:T(8,128)(2,1)}) %reduce-scatter.31.cloned.1.call-update) | async-done | bytes 1048592 | tf_op jit(solution)/shard_map/reduce_scatter | solution.py:214
  3221.5 66.9 %all-gather.49.cloned.1.call-done = bf16[1024,2048]{1,0:T(8,128)(2,1)} async-done(((bf16[256,2048]{1,0:T(8,128)(2,1)}), bf16[1024,2048]{1,0:T(8,128)(2,1)}) %all-gather.49.cloned.1.call-update) | async-done | bytes 4194320 | tf_op jit(solution)/shard_map/all_gather | solution.py:156
  3288.4 19.9 fusion.365
  3308.2 61.5 %all-gather.47.cloned.1.call-done = bf16[1024,2048]{1,0:T(8,128)(2,1)} async-done(((bf16[256,2048]{1,0:T(8,128)(2,1)}), bf16[1024,2048]{1,0:T(8,128)(2,1)}) %all-gather.47.cloned.1.call-update) | async-done | bytes 4194320 | tf_op jit(solution)/shard_map/all_gather | solution.py:169
  3404.6 20.7 fusion.122
  3454.2 25.1 reduce-scatter.33.cloned.1.call-done
  3487.6 60.5 %while.319 = (s32[]{:T(128)}, f32[4,128,128]{2,1,0:T(8,128)S(1)}, f32[16,4,128,128]{3,2,1,0:T(8,128)}, f32[16,4,128,1]{2,1,3,0:T(4,128)}, f32[16,4,128]{2,1,0:T(...) while((s32[]{:T(128)}, f32[4,128,128]{2,1,0:T(8,128)S(1)}, ...), condition=%wide.region_118.119_spmd.clone, body=%wide.region_117.118_spmd.clone.sunk | while | flops 262147 | bytes 1845368 | solution.py:68
  3594.5 20.5 fusion.121
  3675.2 196.5 %while.308 = (s32[]{:T(128)}, f32[2,8,64,4,128]{4,2,3,1,0:T(8,128)}, f32[2,8,64,4,128]{4,2,3,1,0:T(8,128)}, f32[2,8,64,4,128]{4,2,3,1,0:T(8,128)}, f32[2,8,64,4,...) while((s32[]{:T(128)}, f32[2,8,64,4,128]{4,2,3,1,0:T(8,128)}, ...), condition=%wide.region_116.117_spmd, body=%wide.region_110.116_spmd.sunk | while | flops 754327552 | bytes 107512264 | solution.py:78
  3687.4 77.3 %fusion.528 = (f32[8,64,4,128]{3,1,2,0:T(8,128)}, f32[8,64,4,128]{3,2,1,0:T(4,128)}, f32[8,64,4,128]{3,2,1,0:T(4,128)}, f32[8,64,64,4]{2,3,1,0:T(4,128)}, f32[8,64,4,128]{3,1,2,0:T(8,128)}) fusion(f32[8,64,4,128]{3,2,1,0:T(4,128)} %dynamic-slice_bitcast_fusion.80, f32[8,64,4,128]{3,1,2,0:T(8,128)} %dynamic-slice_bitcast_fusion.81, ...), kind=kLoop, calls=%fused_computation.164.clone.1 | loop fusion | flops 351141888 | bytes 9453568 | tf_op jit(solution)/shard_map/transpose(jvp())/while/body/eval_jaxpr/checkpoint/reduce_sum | solution.py:41
  3785.5 77.3 %fusion.528 = (f32[8,64,4,128]{3,1,2,0:T(8,128)}, f32[8,64,4,128]{3,2,1,0:T(4,128)}, f32[8,64,4,128]{3,2,1,0:T(4,128)}, f32[8,64,64,4]{2,3,1,0:T(4,128)}, f32[8,64,4,128]{3,1,2,0:T(8,128)}) fusion(f32[8,64,4,128]{3,2,1,0:T(4,128)} %dynamic-slice_bitcast_fusion.80, f32[8,64,4,128]{3,1,2,0:T(8,128)} %dynamic-slice_bitcast_fusion.81, ...), kind=kLoop, calls=%fused_computation.164.clone.1 | loop fusion | flops 351141888 | bytes 9453568 | tf_op jit(solution)/shard_map/transpose(jvp())/while/body/eval_jaxpr/checkpoint/reduce_sum | solution.py:41
  3885.6 43.6 while.320
  4009.8 25.1 add_convert_fusion
  4079.8 74.9 %all-reduce.12 = (f32[1,2048]{1,0:T(1,128)}, f32[1,2048]{1,0:T(1,128)}) all-reduce(f32[1,2048]{1,0:T(1,128)S(1)} %bitcast.1141, f32[1,2048]{1,0:T(1,128)S(1)} %bitcast.1140), channel_id=1, replica_groups=mesh['pipe'=2,'seq'=4,'dp'=4] {'seq','dp'}, use_global_device_ids=true, to_apply=%region_129.130 | all-reduce | flops 4096 | bytes 32768 | tf_op jit(solution)/shard_map/psum | solution.py:321
  4160.8 363.9 %all-reduce.20.cloned.1.call-done = (bf16[2048,1536]{1,0:T(8,128)(2,1)}, bf16[1,512,2048]{2,1,0:T(8,128)(2,1)}, bf16[2048,2816]{1,0:T(8,128)(2,1)}, bf16[1,1408,2048]{2,1,0:T(8,128)(2,1)}) async-done(((bf16[2048,1536]{1,0:T(8,128)(2,1)}, bf16[1,512,2048]{2,1,0:T(8,128)(2,1)}, bf16[2048,2816]{1,0:T(8,128)(2,1)}, bf16[1,1408,2048]{2,1,0:T(8,128)(2,1)}), (bf16[2048,1536]{1,0:T(8,128)(2,1)}, ...) | async-done | bytes 25690128 | tf_op jit(solution)/shard_map/psum | solution.py:88
  (2125 shorter events, 2076.2 us)
Async XLA Ops:
  7.2 457.6 %copy-start = (s32[2,4]{1,0:T(2,128)S(1)}, s32[2,4]{1,0:T(2,128)}, u32[]{:S(2)}) copy-start(s32[2,4]{1,0:T(2,128)} %param.58) | copy-start | bytes 100
  7.2 87.8 %all-gather.19.cloned.1.call-start = ((), (), s32[]{:S(2)}) async-start(), calls=%async_computation.12 | async-start | bytes 5242880 | tf_op jit(solution)/shard_map/all_gather | solution.py:146
  11.4 336.2 %reduce-scatter.13.cloned.1.call-start = ((), (), s32[]{:S(2)}) async-start(), calls=%async_computation.13 | async-start | bytes 5242880 | tf_op jit(solution)/shard_map/reduce_scatter | solution.py:254
  15.5 89.2 %copy-start.238 = (f32[1,512]{1,0:T(1,128)}, f32[1,512]{1,0:T(1,128)S(1)}, u32[]{:S(2)}) copy-start(f32[1,512]{1,0:T(1,128)S(1)} %broadcast_subtract_fusion) | copy-start | bytes 6148
  271.6 160.7 %all-gather.21.cloned.1.call-start = ((), (), s32[]{:S(2)}) async-start(), calls=%async_computation.14 | async-start | bytes 5242880 | tf_op jit(solution)/shard_map/all_gather | solution.py:156
  350.9 189.3 %reduce-scatter.15.cloned.1.call-start = ((), (), s32[]{:S(2)}) async-start(), calls=%async_computation.15 | async-start | bytes 5242880 | tf_op jit(solution)/shard_map/reduce_scatter | solution.py:265
  464.7 166.0 %all-gather.23.cloned.1.call-start = ((), (), s32[]{:S(2)}) async-start(), calls=%async_computation.16 | async-start | bytes 5242880 | tf_op jit(solution)/shard_map/all_gather | solution.py:146
  542.1 3.8 collective-permute-start
  549.1 81.7 %copy-start.165 = (bf16[2048,512]{1,0:T(8,128)(2,1)S(1)}, bf16[2048,512]{1,0:T(8,128)(2,1)}, u32[]{:S(2)}) copy-start(bf16[2048,512]{1,0:T(8,128)(2,1)} %copy-done.164) | copy-start | bytes 6291460
  549.1 162.9 %all-gather.35.cloned.1.call-start = ((), (), s32[]{:S(2)}) async-start(), calls=%async_computation.27 | async-start | bytes 5242880 | tf_op jit(solution)/shard_map/all_gather | solution.py:146
  549.7 585.1 %reduce-scatter.17.cloned.1.call-start = ((), (), s32[]{:S(2)}) async-start(), calls=%async_computation.17 | async-start | bytes 5242880 | tf_op jit(solution)/shard_map/reduce_scatter | solution.py:254
  642.3 79.5 %copy-start.233 = (f32[1,512]{1,0:T(1,128)S(1)}, f32[1,512]{1,0:T(1,128)}, u32[]{:S(2)}) copy-start(f32[1,512]{1,0:T(1,128)} %param.63) | copy-start | bytes 6148
  642.3 79.5 %copy-start.239 = (f32[1,512]{1,0:T(1,128)S(1)}, f32[1,512]{1,0:T(1,128)}, u32[]{:S(2)}) copy-start(f32[1,512]{1,0:T(1,128)} %copy-done.238) | copy-start | bytes 6148
  766.8 267.1 %copy-start.2 = (f32[16,64,4,128]{3,0,1,2:T(8,128)}, f32[16,64,4,128]{3,0,1,2:T(8,128)S(1)}, u32[]{:S(2)}) copy-start(f32[16,64,4,128]{3,0,1,2:T(8,128)S(1)} %fusion.250) | copy-start | bytes 6291460
  1052.8 295.1 %copy-start.261 = (f32[1024]{0:T(1024)}, f32[1024]{0:T(1024)S(1)}, u32[]{:S(2)}) copy-start(f32[1024]{0:T(1024)S(1)} %get-tuple-element.2397) | copy-start | bytes 12292
  1058.9 160.6 %all-gather.25.cloned.1.call-start = ((), (), s32[]{:S(2)}) async-start(), calls=%async_computation.18 | async-start | bytes 5242880 | tf_op jit(solution)/shard_map/all_gather | solution.py:156
  1138.1 189.4 %reduce-scatter.19.cloned.1.call-start = ((), (), s32[]{:S(2)}) async-start(), calls=%async_computation.19 | async-start | bytes 5242880 | tf_op jit(solution)/shard_map/reduce_scatter | solution.py:265
  1252.1 167.3 %all-gather.27.cloned.1.call-start = ((), (), s32[]{:S(2)}) async-start(), calls=%async_computation.20 | async-start | bytes 5242880 | tf_op jit(solution)/shard_map/all_gather | solution.py:146
  1253.4 89.0 %copy-start.285 = (f32[256]{0:T(256)}, f32[256]{0:T(256)S(1)}, u32[]{:S(2)}) copy-start(f32[256]{0:T(256)S(1)} %get-tuple-element.2523) | copy-start | bytes 3076
  1330.8 3.7 collective-permute-start.1
  1337.7 163.1 %all-gather.43.cloned.1.call-start = ((), (), s32[]{:S(2)}) async-start(), calls=%async_computation.33 | async-start | bytes 5242880 | tf_op jit(solution)/shard_map/all_gather | solution.py:146
  1341.0 346.8 %all-gather.33.cloned.1.call-start = ((), (), s32[]{:S(2)}) async-start(), calls=%async_computation.25 | async-start | bytes 5242880 | tf_op jit(solution)/shard_map/all_gather | solution.py:156
  1342.3 365.2 %all-gather.31.cloned.1.call-start = ((), (), s32[]{:S(2)}) async-start(), calls=%async_computation.24 | async-start | bytes 5242880 | tf_op jit(solution)/shard_map/all_gather | solution.py:169
  1345.0 472.3 %reduce-scatter.25.cloned.1.call-start = ((), (), s32[]{:S(2)}) async-start(), calls=%async_computation.26 | async-start | bytes 5242880 | tf_op jit(solution)/shard_map/reduce_scatter | solution.py:184
  1412.1 88.7 %copy-start.166 = (bf16[2048,512]{1,0:T(8,128)(2,1)S(1)}, bf16[2048,512]{1,0:T(8,128)(2,1)}, u32[]{:S(2)}) copy-start(bf16[2048,512]{1,0:T(8,128)(2,1)} %copy-done.164) | copy-start | bytes 6291460
  1687.1 206.2 %copy-start.4 = (f32[16,64,4,128]{3,0,1,2:T(8,128)}, f32[16,64,4,128]{3,0,1,2:T(8,128)S(1)}, u32[]{:S(2)}) copy-start(f32[16,64,4,128]{3,0,1,2:T(8,128)S(1)} %fusion.246) | copy-start | bytes 6291460
  1742.1 163.8 %all-gather.37.cloned.1.call-start = ((), (), s32[]{:S(2)}) async-start(), calls=%async_computation.28 | async-start | bytes 5242880 | tf_op jit(solution)/shard_map/all_gather | solution.py:196
  1824.4 436.9 %reduce-scatter.21.cloned.1.call-start = ((), (), s32[]{:S(2)}) async-start(), calls=%async_computation.21 | async-start | bytes 5242880 | tf_op jit(solution)/shard_map/reduce_scatter | solution.py:254
  1945.8 390.7 %reduce-scatter.27.cloned.1.call-start = ((), (), s32[]{:S(2)}) async-start(), calls=%async_computation.29 | async-start | bytes 5242880 | tf_op jit(solution)/shard_map/reduce_scatter | solution.py:214
  1952.2 196.4 %copy-start.3 = (f32[16,64,4,128]{3,0,1,2:T(8,128)S(1)}, f32[16,64,4,128]{3,0,1,2:T(8,128)}, u32[]{:S(2)}) copy-start(f32[16,64,4,128]{3,0,1,2:T(8,128)} %copy-done.2) | copy-start | bytes 6291460
  2261.3 78.3 %copy-start.24 = (bf16[256,2048]{1,0:T(8,128)(2,1)S(1)}, bf16[256,2048]{1,0:T(8,128)(2,1)}, u32[]{:S(2)}) copy-start(bf16[256,2048]{1,0:T(8,128)(2,1)} %copy-done.22) | copy-start | bytes 3145732
  2261.3 78.3 %copy-start.200 = (f32[1,2048]{1,0:T(1,128)S(1)}, f32[1,2048]{1,0:T(1,128)}, u32[]{:S(2)}) copy-start(f32[1,2048]{1,0:T(1,128)} %param.66) | copy-start | bytes 24580
  2261.3 167.2 %all-gather.51.cloned.1.call-start = ((), (), s32[]{:S(2)}) async-start(), calls=%async_computation.39 | async-start | bytes 5242880 | tf_op jit(solution)/shard_map/all_gather | solution.py:146
  2347.1 162.8 %all-gather.41.cloned.1.call-start = ((), (), s32[]{:S(2)}) async-start(), calls=%async_computation.31 | async-start | bytes 5242880 | tf_op jit(solution)/shard_map/all_gather | solution.py:156
  2347.1 61.6 %collective-permute-start.2 = (bf16[256,2048]{1,0:T(8,128)(2,1)}, bf16[256,2048]{1,0:T(8,128)(2,1)}, u32[]{:S(2)}, u32[]{:S(2)}) collective-permute-start(bf16[256,2048]{1,0:T(8,128)(2,1)} %get-tuple-element.2511), channel_id=1, source_target_pairs={{16,0},{17,1},{18,2},{19,3},{20,4},{21,5},{22,6},{23,7},{24,8},{25... | collective-permute-start | bytes 3145736 | tf_op jit(solution)/shard_map/ppermute | solution.py:22
  2351.9 238.7 %all-gather.39.cloned.1.call-start = ((), (), s32[]{:S(2)}) async-start(), calls=%async_computation.30 | async-start | bytes 5242880 | tf_op jit(solution)/shard_map/all_gather | solution.py:169
  2411.5 288.9 %reduce-scatter.29.cloned.1.call-start = ((), (), s32[]{:S(2)}) async-start(), calls=%async_computation.32 | async-start | bytes 5242880 | tf_op jit(solution)/shard_map/reduce_scatter | solution.py:184
  2464.5 312.0 %copy-start.6 = (f32[16,64,4,128]{3,0,1,2:T(8,128)}, f32[16,64,4,128]{3,0,1,2:T(8,128)S(1)}, u32[]{:S(2)}) copy-start(f32[16,64,4,128]{3,0,1,2:T(8,128)S(1)} %fusion.242) | copy-start | bytes 6291460
  2624.9 164.3 %all-gather.45.cloned.1.call-start = ((), (), s32[]{:S(2)}) async-start(), calls=%async_computation.34 | async-start | bytes 5242880 | tf_op jit(solution)/shard_map/all_gather | solution.py:196
  2707.8 497.8 %reduce-scatter.31.cloned.1.call-start = ((), (), s32[]{:S(2)}) async-start(), calls=%async_computation.35 | async-start | bytes 5242880 | tf_op jit(solution)/shard_map/reduce_scatter | solution.py:214
  2821.1 196.5 %copy-start.5 = (f32[16,64,4,128]{3,0,1,2:T(8,128)S(1)}, f32[16,64,4,128]{3,0,1,2:T(8,128)}, u32[]{:S(2)}) copy-start(f32[16,64,4,128]{3,0,1,2:T(8,128)} %copy-done.4) | copy-start | bytes 6291460
  3130.0 78.9 %copy-start.274 = (f32[256]{0:T(256)S(1)}, f32[256]{0:T(256)}, u32[]{:S(2)}) copy-start(f32[256]{0:T(256)} %copy-done.273) | copy-start | bytes 3076
  3130.0 78.9 %copy-start.57 = (bf16[256,2048]{1,0:T(8,128)(2,1)S(1)}, bf16[256,2048]{1,0:T(8,128)(2,1)}, u32[]{:S(2)}) copy-start(bf16[256,2048]{1,0:T(8,128)(2,1)} %copy-done.54) | copy-start | bytes 3145732
  3130.0 78.9 %copy-start.87 = (f32[256,2048]{1,0:T(8,128)S(1)}, f32[256,2048]{1,0:T(8,128)}, u32[]{:S(2)}) copy-start(f32[256,2048]{1,0:T(8,128)} %get-tuple-element.2419) | copy-start | bytes 6291460
  3130.0 78.9 %copy-start.254 = (f32[256]{0:T(256)S(1)}, f32[256]{0:T(256)}, u32[]{:S(2)}) copy-start(f32[256]{0:T(256)} %copy-done.252) | copy-start | bytes 3076
  3130.0 78.9 %copy-start.284 = (f32[256]{0:T(256)S(1)}, f32[256]{0:T(256)}, u32[]{:S(2)}) copy-start(f32[256]{0:T(256)} %copy-done.283) | copy-start | bytes 3076
  3130.0 158.3 %all-gather.49.cloned.1.call-start = ((), (), s32[]{:S(2)}) async-start(), calls=%async_computation.37 | async-start | bytes 5242880 | tf_op jit(solution)/shard_map/all_gather | solution.py:156
  3130.6 239.1 %all-gather.47.cloned.1.call-start = ((), (), s32[]{:S(2)}) async-start(), calls=%async_computation.36 | async-start | bytes 5242880 | tf_op jit(solution)/shard_map/all_gather | solution.py:169
  3215.6 4.6 collective-permute-start.3
  3220.1 261.9 %copy-start.116 = (bf16[256,2048]{1,0:T(8,128)(2,1)}, bf16[256,2048]{1,0:T(8,128)(2,1)S(1)}, u32[]{:S(2)}) copy-start(bf16[256,2048]{1,0:T(8,128)(2,1)S(1)} %collective-permute-done.3) | copy-start | bytes 3145732
  3221.5 257.9 %reduce-scatter.33.cloned.1.call-start = ((), (), s32[]{:S(2)}) async-start(), calls=%async_computation.38 | async-start | bytes 5242880 | tf_op jit(solution)/shard_map/reduce_scatter | solution.py:184
  3403.9 158.1 %all-gather.29.cloned.1.call-start = ((), (), s32[]{:S(2)}) async-start(), calls=%async_computation.22 | async-start | bytes 5242880 | tf_op jit(solution)/shard_map/all_gather | solution.py:156
  3404.5 239.5 %all-gather.53.cloned.1.call-start = ((), (), s32[]{:S(2)}) async-start(), calls=%async_computation.40 | async-start | bytes 5242880 | tf_op jit(solution)/shard_map/all_gather | solution.py:196
  3484.4 575.5 %reduce-scatter.23.cloned.1.call-start = ((), (), s32[]{:S(2)}) async-start(), calls=%async_computation.23 | async-start | bytes 5242880 | tf_op jit(solution)/shard_map/reduce_scatter | solution.py:265
  3551.0 109.8 %copy-start.76 = (f32[16,64,4,128]{3,2,1,0:T(4,128)}, f32[16,64,4,128]{3,2,1,0:T(4,128)S(1)}, u32[]{:S(2)}) copy-start(f32[16,64,4,128]{3,2,1,0:T(4,128)S(1)} %copy.379) | copy-start | bytes 6291460
  3594.5 482.7 %reduce-scatter.35.cloned.1.call-start = ((), (), s32[]{:S(2)}) async-start(), calls=%async_computation.41 | async-start | bytes 5242880 | tf_op jit(solution)/shard_map/reduce_scatter | solution.py:214
  3675.2 196.5 %copy-start.7 = (f32[16,64,4,128]{3,0,1,2:T(8,128)S(1)}, f32[16,64,4,128]{3,0,1,2:T(8,128)}, u32[]{:S(2)}) copy-start(f32[16,64,4,128]{3,0,1,2:T(8,128)} %copy-done.6) | copy-start | bytes 6291460
  3990.1 534.6 %all-reduce.20.cloned.1.call-start = ((), (), s32[]{:S(2)}) async-start(), calls=%async_computation.42 | async-start | bytes 51380224 | tf_op jit(solution)/shard_map/psum | solution.py:88
  4065.6 89.1 %copy-start.288 = (f32[256]{0:T(256)S(1)}, f32[256]{0:T(256)}, u32[]{:S(2)}) copy-start(f32[256]{0:T(256)} %copy-done.287) | copy-start | bytes 3076
  4065.6 89.2 %copy-start.27 = (f32[256,2048]{1,0:T(8,128)S(1)}, f32[256,2048]{1,0:T(8,128)}, u32[]{:S(2)}) copy-start(f32[256,2048]{1,0:T(8,128)} %copy-done.25) | copy-start | bytes 6291460
  4065.6 89.2 %copy-start.202 = (f32[1,2048]{1,0:T(1,128)S(1)}, f32[1,2048]{1,0:T(1,128)}, u32[]{:S(2)}) copy-start(f32[1,2048]{1,0:T(1,128)} %param.66) | copy-start | bytes 24580
  4065.6 89.2 %copy-start.257 = (f32[256]{0:T(256)S(1)}, f32[256]{0:T(256)}, u32[]{:S(2)}) copy-start(f32[256]{0:T(256)} %copy-done.255) | copy-start | bytes 3076
  4065.6 89.2 %copy-start.271 = (f32[256]{0:T(256)S(1)}, f32[256]{0:T(256)}, u32[]{:S(2)}) copy-start(f32[256]{0:T(256)} %get-tuple-element.2522) | copy-start | bytes 3076
  4065.6 89.2 %copy-start.292 = (f32[256]{0:T(256)S(1)}, f32[256]{0:T(256)}, u32[]{:S(2)}) copy-start(f32[256]{0:T(256)} %copy-done.291) | copy-start | bytes 3076
  (308 other events, 3420.0 us)
Sparse Core Ops, SparseCore 0:
  11.5 83.4 all-gather.18
  271.7 75.8 reduce-scatter.12
  351.0 81.2 all-gather.20
  464.9 75.2 reduce-scatter.14
  549.2 81.4 all-gather.22
  632.7 79.2 all-gather.34
  1059.0 75.7 reduce-scatter.16
  1138.2 81.2 all-gather.24
  1252.2 75.2 reduce-scatter.18
  1337.8 81.4 all-gather.26
  1421.5 79.2 all-gather.42
  1502.2 79.2 all-gather.32
  1583.0 79.2 all-gather.30
  1742.2 75.0 reduce-scatter.24
  1824.6 81.2 all-gather.36
  1945.9 75.1 reduce-scatter.20
  2261.4 75.1 reduce-scatter.26
  2347.2 81.2 all-gather.50
  2430.6 79.2 all-gather.40
  2511.3 79.2 all-gather.38
  2625.1 75.2 reduce-scatter.28
  2707.9 81.2 all-gather.44
  3130.1 75.4 reduce-scatter.30
  3207.1 81.2 all-gather.48
  3290.5 79.2 all-gather.46
  3404.0 75.2 reduce-scatter.32
  3480.8 81.2 all-gather.28
  3563.6 79.2 all-gather.52
  3645.7 75.5 reduce-scatter.22
  3990.2 76.5 reduce-scatter.34
  4071.3 453.3 all-reduce.19
where the time goes:
time: 4600 us; the launch traced here: 4580 us
  waiting for transfers between devices  1610 us (35%)
  other arithmetic  1370 us (30%)
  matrix products  842 us (18%)
  local copies, waits for them, and re-layouts  582 us (13%)
  blocking collectives  140 us (3%)
    reduce_sum x6, other arithmetic, intra_part(): differ = cumul[:, :, None] - cumul[:, None, :]  464 us
    psum x1, waiting for transfers between devices, sum_grads(): lax.psum(shortened(weight_grads), 'dp')  364 us
    all_gather x6, waiting for transfers between devices, mixer_front(): normed_all = lax.all_gather(normed, 'seq', axis=0, tiled=True)  316 us
    reduce_sum x12, other arithmetic, intra_part(): jnp.sum(weight * query_blocks[:, :, None] * key_blocks[:, None, :], axis=-1)  292 us
    all_gather x6, waiting for transfers between devices, ffn_front(): normed_two_all = lax.all_gather(normed_two, 'seq', axis=0, tiled=True)  249 us
    add x144, other arithmetic, advance(): return (decay[..., None] * state + update, state)  157 us
    reduce_scatter x3, waiting for transfers between devices, body(): lax.psum_scatter(jnp.dot(forward_head_normed, w_out, preferred_element_ty...  152 us
    reduce_scatter x3, waiting for transfers between devices, body(): lax.psum_scatter(jnp.dot(forward_hidden, w_down_local, preferred_element_...  149 us
  transfers between devices with their start and end apart: 35, of which 28 were waited for; matrix products, arithmetic and copies ran while one was open for 36% of the time, Pallas kernels for 0%

commit v1 on v0

v1 whole, which is shorter than its diff:
```python
import jax
import jax.numpy as jnp
from jax import lax
from jax.experimental import pallas as pl
from jax.experimental.pallas import tpu as pltpu
from jax.sharding import PartitionSpec as P

EPSILON = 1e-06
SPAN = 128
HEAD = 128
HIGH = lax.Precision.HIGHEST


def mm(a, b, ca, cb):
    return lax.dot_general(
        a.astype(jnp.bfloat16),
        b.astype(jnp.bfloat16),
        (((ca,), (cb,)), ((), ())),
        preferred_element_type=jnp.float32,
    )


def gates(raw, lb):
    small = jnp.exp(-jnp.abs(raw))
    inv = 1.0 / (1.0 + small)
    sig = jnp.where(raw >= 0, inv, small * inv)
    nsig = jnp.where(raw >= 0, small * inv, inv)
    forget = lb + (1.0 - lb) * sig
    return sig, nsig, forget


def lower_mask():
    rows = lax.broadcasted_iota(jnp.int32, (SPAN, SPAN), 0)
    cols = lax.broadcasted_iota(jnp.int32, (SPAN, SPAN), 1)
    return rows >= cols


def rec_fwd_kernel(proj_ref, lb_ref, gain_ref, mg_ref, sq_ref, st_ref, state):
    width = lb_ref.shape[1]

    @pl.when(pl.program_id(0) == 0)
    def _():
        state[...] = jnp.zeros_like(state)

    lb = lb_ref[...]
    causal = lower_mask()
    _, nsig, forget = gates(proj_ref[:, width : 2 * width], lb)
    keys = (1.0 - lb) * nsig
    cumul = lax.dot_general(
        causal.astype(jnp.float32),
        jnp.log(forget),
        (((1,), (0,)), ((), ())),
        precision=HIGH,
        preferred_element_type=jnp.float32,
    )
    middle = cumul[SPAN // 2 - 1 : SPAN // 2]
    ending = cumul[SPAN - 1 : SPAN]
    to_mid = jnp.exp(middle)
    to_end = jnp.exp(ending - middle)
    decay = jnp.exp(ending)
    q_mid = proj_ref[:, :width] * jnp.exp(cumul - middle)
    k_mid = keys * jnp.exp(middle - cumul)
    q_start = q_mid * to_mid
    k_end = k_mid * to_end
    total = jnp.zeros((8, SPAN), jnp.float32)
    ones = jnp.ones((8, HEAD), jnp.float32)
    for head in range(width // HEAD):
        cut = slice(head * HEAD, (head + 1) * HEAD)
        vals = proj_ref[:, 2 * width + head * HEAD : 2 * width + (head + 1) * HEAD]
        before = state[head]
        st_ref[0, head] = before
        scores = jnp.where(causal, mm(q_mid[:, cut], k_mid[:, cut], 1, 1), 0.0)
        mixed = mm(scores, vals, 1, 0) + mm(q_start[:, cut], before, 1, 1)
        state[head] = decay[:, cut] * before + mm(vals, k_end[:, cut], 0, 0)
        total += lax.dot_general(
            ones,
            mixed * mixed,
            (((1,), (1,)), ((), ())),
            precision=HIGH,
            preferred_element_type=jnp.float32,
        )
        mg_ref[:, cut] = (mixed * gain_ref[:, cut]).astype(jnp.bfloat16)
    sq_ref[...] = total


def rec_bwd_kernel(proj_ref, st_ref, dm_ref, lb_ref, dproj_ref, glb_ref, dstate):
    width = lb_ref.shape[1]

    @pl.when(pl.program_id(0) == 0)
    def _():
        dstate[...] = jnp.zeros_like(dstate)
        glb_ref[...] = jnp.zeros_like(glb_ref)

    lb = lb_ref[...]
    causal = lower_mask()
    lower = causal.astype(jnp.float32)
    sig, nsig, forget = gates(proj_ref[:, width : 2 * width], lb)
    keys = (1.0 - lb) * nsig
    cumul = lax.dot_general(
        lower,
        jnp.log(forget),
        (((1,), (0,)), ((), ())),
        precision=HIGH,
        preferred_element_type=jnp.float32,
    )
    middle = cumul[SPAN // 2 - 1 : SPAN // 2]
    ending = cumul[SPAN - 1 : SPAN]
    to_mid = jnp.exp(middle)
    to_end = jnp.exp(ending - middle)
    decay = jnp.exp(ending)
    eq = jnp.exp(cumul - middle)
    ek = jnp.exp(middle - cumul)
    q_mid = (proj_ref[:, :width] * eq).astype(jnp.bfloat16)
    k_mid = (keys * ek).astype(jnp.bfloat16)
    for head in range(width // HEAD):
        cut = slice(head * HEAD, (head + 1) * HEAD)
        vals = proj_ref[:, 2 * width + head * HEAD : 2 * width + (head + 1) * HEAD].astype(
            jnp.bfloat16
        )
        qm, km = q_mid[:, cut], k_mid[:, cut]
        qf, kf = qm.astype(jnp.float32), km.astype(jnp.float32)
        qs = qf * to_mid[:, cut]
        ke = kf * to_end[:, cut]
        before = st_ref[0, head]
        after = dstate[head]
        dmix = dm_ref[:, cut]
        scores = jnp.where(causal, mm(qm, km, 1, 1), 0.0)
        dscores = jnp.where(causal, mm(dmix, vals, 1, 1), 0.0).astype(jnp.bfloat16)
        dq_in = mm(dscores, km, 1, 0)
        dk_in = mm(dscores, qm, 0, 0)
        dq_out = mm(dmix, before, 1, 0)
        dk_out = mm(vals, after, 1, 0)
        dvals = mm(scores, dmix, 0, 0) + mm(ke, after, 1, 1)
        flow = ke * dk_out
        change = qf * dq_in - kf * dk_in + qs * dq_out - flow
        edge = jnp.sum(flow, axis=0, keepdims=True) + decay[:, cut] * jnp.sum(
            before * after, axis=0, keepdims=True
        )
        dlog = (
            lax.dot_general(
                lower,
                change,
                (((0,), (0,)), ((), ())),
                precision=HIGH,
                preferred_element_type=jnp.float32,
            )
            + edge
        )
        dqueries = eq[:, cut] * (dq_in + to_mid[:, cut] * dq_out)
        dkeys = ek[:, cut] * (dk_in + to_end[:, cut] * dk_out)
        lbh, sg, ns = lb[:, cut], sig[:, cut], nsig[:, cut]
        ratio = dlog / forget[:, cut] - dkeys
        draw = ratio * ((1.0 - lbh) * sg * ns)
        glb_ref[:, cut] += jnp.broadcast_to(
            jnp.sum(ratio * ns, axis=0, keepdims=True), (8, HEAD)
        )
        dstate[head] = decay[:, cut] * after + mm(dmix, qs, 0, 0)
        dproj_ref[:, cut] = dqueries.astype(jnp.bfloat16)
        dproj_ref[:, width + head * HEAD : width + (head + 1) * HEAD] = draw.astype(jnp.bfloat16)
        dproj_ref[:, 2 * width + head * HEAD : 2 * width + (head + 1) * HEAD] = dvals.astype(
            jnp.bfloat16
        )


def rec_fwd(proj, lb, gain):
    length, width = proj.shape[0], lb.shape[0]
    spans, heads = length // SPAN, width // HEAD
    return pl.pallas_call(
        rec_fwd_kernel,
        grid=(spans,),
        in_specs=[
            pl.BlockSpec((SPAN, 3 * width), lambda i: (i, 0)),
            pl.BlockSpec((1, width), lambda i: (0, 0)),
            pl.BlockSpec((1, width), lambda i: (0, 0)),
        ],
        out_specs=[
            pl.BlockSpec((SPAN, width), lambda i: (i, 0)),
            pl.BlockSpec((8, SPAN), lambda i: (0, i)),
            pl.BlockSpec((1, heads, HEAD, HEAD), lambda i: (i, 0, 0, 0)),
        ],
        out_shape=[
            jax.ShapeDtypeStruct((length, width), jnp.bfloat16),
            jax.ShapeDtypeStruct((8, length), jnp.float32),
            jax.ShapeDtypeStruct((spans, heads, HEAD, HEAD), jnp.float32),
        ],
        scratch_shapes=[pltpu.VMEM((heads, HEAD, HEAD), jnp.float32)],
        cost_estimate=pl.CostEstimate(
            flops=8 * length * SPAN * width,
            bytes_accessed=20 * length * width,
            transcendentals=8 * length * width,
        ),
        name="rec_fwd",
    )(proj, lb[None], gain[None])


def rec_bwd(proj, states, dmix, lb):
    length, width = proj.shape[0], lb.shape[0]
    spans, heads = length // SPAN, width // HEAD
    dproj, glb = pl.pallas_call(
        rec_bwd_kernel,
        grid=(spans,),
        in_specs=[
            pl.BlockSpec((SPAN, 3 * width), lambda i: (spans - 1 - i, 0)),
            pl.BlockSpec((1, heads, HEAD, HEAD), lambda i: (spans - 1 - i, 0, 0, 0)),
            pl.BlockSpec((SPAN, width), lambda i: (spans - 1 - i, 0)),
            pl.BlockSpec((1, width), lambda i: (0, 0)),
        ],
        out_specs=[
            pl.BlockSpec((SPAN, 3 * width), lambda i: (spans - 1 - i, 0)),
            pl.BlockSpec((8, width), lambda i: (0, 0)),
        ],
        out_shape=[
            jax.ShapeDtypeStruct((length, 3 * width), jnp.bfloat16),
            jax.ShapeDtypeStruct((8, width), jnp.float32),
        ],
        scratch_shapes=[pltpu.VMEM((heads, HEAD, HEAD), jnp.float32)],
        cost_estimate=pl.CostEstimate(
            flops=20 * length * SPAN * width,
            bytes_accessed=30 * length * width,
            transcendentals=8 * length * width,
        ),
        name="rec_bwd",
    )(proj, states, dmix, lb[None])
    return dproj, glb[0]


def other_core(array):
    return lax.ppermute(array, "pipe", [(0, 1), (1, 0)])


def small_sum(array, axis):
    size = lax.axis_size(axis)
    if size > 4:
        return lax.psum(array, axis)
    total = array
    for step in range(1, size):
        total = total + lax.ppermute(array, axis, [(i, (i + step) % size) for i in range(size)])
    return total


def pick(first, zero, one):
    return jnp.where(first, zero, one)


def inverse_rms(values_in):
    return lax.rsqrt(jnp.mean(values_in * values_in, axis=-1, keepdims=True) + EPSILON)


def norm_backward(values_in, gain, grad):
    inv = inverse_rms(values_in)
    unit = values_in * inv
    grad_gain = jnp.sum(grad * unit, axis=0)
    scaled = grad * gain
    return inv * (scaled - unit * jnp.mean(scaled * unit, axis=-1, keepdims=True)), grad_gain


def dot(left, right, left_dim, right_dim, kind=jnp.float32):
    return lax.dot_general(
        left, right, (((left_dim,), (right_dim,)), ((), ())), preferred_element_type=jnp.float32
    ).astype(kind)


def gather_rows(array):
    return lax.all_gather(array, "seq", axis=0, tiled=True)


def scatter_rows(array):
    return lax.psum_scatter(array, "seq", scatter_dimension=0, tiled=True).astype(jnp.float32)


def pair_moves(step):
    count = lax.axis_size("dp")
    return [(i, i ^ step) for i in range(count)]


def start_sum(grad):
    core = lax.axis_index("pipe")
    row = lax.axis_index("dp")
    count = lax.axis_size("dp")
    rows, columns = grad.shape
    halves = grad.reshape(2, rows // 2, columns)
    keep = lax.dynamic_index_in_dim(halves, core, 0, keepdims=False)
    send = lax.dynamic_index_in_dim(halves, 1 - core, 0, keepdims=False)
    half = (
        keep.astype(jnp.float32) + other_core(send).astype(jnp.float32)
    ).astype(jnp.bfloat16)
    parts = half.reshape(count, rows // (2 * count), columns)
    total = lax.dynamic_index_in_dim(parts, row, 0, keepdims=False).astype(jnp.float32)
    for step in range(1, count):
        away = lax.dynamic_index_in_dim(parts, row ^ step, 0, keepdims=False)
        total = total + lax.ppermute(away, "dp", pair_moves(step)).astype(jnp.float32)
    return total.astype(jnp.bfloat16)


def finish_sum(zero, one):
    core = lax.axis_index("pipe")
    row = lax.axis_index("dp")
    count = lax.axis_size("dp")
    first = core == 0
    own = pick(first, zero, one)
    swapped = other_core(pick(first, one, zero))
    rows, columns = own.shape
    whole = jnp.zeros((2, count, rows, columns), jnp.float32)

    def put(whole, piece, half, place):
        return lax.dynamic_update_slice(
            whole, piece.astype(jnp.float32)[None, None], (half, place, 0, 0)
        )

    for half, piece in ((core, own), (1 - core, swapped)):
        whole = put(whole, piece, half, row)
        for step in range(1, count):
            whole = put(whole, lax.ppermute(piece, "dp", pair_moves(step)), half, row ^ step)
    return whole.reshape(2 * count * rows, columns)


def body(
    inputs,
    cotangent,
    lengths,
    norm_gain,
    w_query,
    w_forget,
    w_input,
    lower_bound,
    out_gain,
    w_output,
    ffn_gain,
    w_gate,
    w_up,
    w_down,
):
    local_rows, width = inputs.shape[2], inputs.shape[3]
    local_width = w_query.shape[2]
    hidden_here = w_gate.shape[2]
    core = lax.axis_index("pipe")
    row = lax.axis_index("dp")
    place = lax.axis_index("seq")
    first = core == 0
    bf16 = jnp.bfloat16

    def both(array):
        return lax.all_gather(array, "pipe", axis=0, tiled=False)

    w_proj_both = both(jnp.concatenate([w_query[0], w_forget[0], w_input[0]], axis=1).astype(bf16))
    w_out_both = both(w_output[0].astype(bf16))
    w_pair_both = both(jnp.concatenate([w_gate[0], w_up[0]], axis=1).astype(bf16))
    w_down_both = both(w_down[0].astype(bf16))
    gains = both(jnp.stack([norm_gain[0], ffn_gain[0]]))
    bounds = both(jnp.stack([lower_bound[0], out_gain[0]]))

    own_length = lax.dynamic_slice(lengths, (core, row), (1, 1))[0, 0]
    positions = place * local_rows + jnp.arange(local_rows, dtype=jnp.int32)
    mask = (positions < own_length).astype(jnp.float32)[:, None]
    block_in = lax.dynamic_index_in_dim(inputs, core, 0, keepdims=False)[0]
    source_grad = lax.dynamic_index_in_dim(cotangent, core, 0, keepdims=False)[0]

    saved = []
    outs = []
    for section in range(2):
        residual = block_in.astype(jnp.float32)
        normed = (residual * inverse_rms(residual) * gains[section, 0]).astype(bf16)
        normed_all = gather_rows(normed)
        projected = dot(normed_all, w_proj_both[section], 1, 0)
        head_gain = bounds[section, 1]
        mixed_gain, squares, states = rec_fwd(projected, bounds[section, 0], head_gain)
        squares = small_sum(squares[0], "seq")
        branch = scatter_rows(dot(mixed_gain, w_out_both[section], 1, 0, bf16))
        own_squares = lax.dynamic_slice(squares, (place * local_rows,), (local_rows,))
        inv_mix = lax.rsqrt(own_squares / width + EPSILON)[:, None]
        branch = branch * inv_mix
        middle = residual + branch
        normed_two = (middle * inverse_rms(middle) * gains[section, 1]).astype(bf16)
        normed_two_all = gather_rows(normed_two)
        paired = dot(normed_two_all, w_pair_both[section], 1, 0, bf16)
        gate_act = paired[:, :hidden_here].astype(jnp.float32)
        up_act = paired[:, hidden_here:].astype(jnp.float32)
        hidden = (jax.nn.silu(gate_act) * up_act).astype(bf16)
        ffn_branch = scatter_rows(dot(hidden, w_down_both[section], 1, 0, bf16))
        out_low = (mask * (middle + ffn_branch)).astype(bf16)
        outs.append(out_low)
        saved.append(
            (residual, normed_all, projected, mixed_gain, states, inv_mix, branch, middle)
            + (normed_two_all, paired, hidden)
        )
        block_in = out_low

    small = [None, None]
    shares = [None, None]
    grad_ins = [None, None]
    grad_out = source_grad.astype(jnp.float32)
    for section in (1, 0):
        residual, normed_all, projected, mixed_gain, states, inv_mix, branch, middle = saved[
            section
        ][:8]
        normed_two_all, paired, hidden = saved[section][8:]
        head_gain = bounds[section, 1]
        masked = mask * grad_out
        grad_branch_all = gather_rows(masked.astype(bf16))
        grad_hidden = dot(grad_branch_all, w_down_both[section], 1, 1)
        gate_act = paired[:, :hidden_here].astype(jnp.float32)
        up_act = paired[:, hidden_here:].astype(jnp.float32)
        sig = jax.nn.sigmoid(gate_act)
        grad_up = grad_hidden * gate_act * sig
        grad_gate = grad_hidden * up_act * sig * (1.0 + gate_act * (1.0 - sig))
        grad_pair = jnp.concatenate([grad_gate.astype(bf16), grad_up.astype(bf16)], axis=1)
        grad_normed_two = scatter_rows(dot(grad_pair, w_pair_both[section], 1, 1, bf16))
        grad_down = dot(hidden, grad_branch_all, 0, 0, bf16)
        grad_pair_weight = dot(normed_two_all, grad_pair, 0, 0, bf16)
        from_norm, grad_gain_two = norm_backward(middle, gains[section, 1], grad_normed_two)
        grad_middle = masked + from_norm
        inner = jnp.sum(grad_middle * branch, axis=1)
        factor = inv_mix[:, 0] * inv_mix[:, 0] * inner / width
        factor_all = small_sum(
            lax.dynamic_update_slice(
                jnp.zeros((local_rows * lax.axis_size("seq"),), jnp.float32),
                factor,
                (place * local_rows,),
            ),
            "seq",
        )
        grad_mix_all = gather_rows((grad_middle * inv_mix).astype(bf16))
        grad_head = dot(grad_mix_all, w_out_both[section], 1, 1)
        mixed = mixed_gain.astype(jnp.float32) / head_gain
        grad_head_gain = jnp.sum(grad_head * mixed, axis=0)
        grad_mixed = (grad_head * head_gain - mixed * factor_all[:, None]).astype(bf16)
        grad_proj, grad_bound = rec_bwd(projected, states, grad_mixed, bounds[section, 0])
        grad_normed = scatter_rows(dot(grad_proj, w_proj_both[section], 1, 1, bf16))
        grad_out_weight = dot(mixed_gain, grad_mix_all, 0, 0, bf16)
        grad_proj_weight = dot(normed_all, grad_proj, 0, 0, bf16)
        from_first, grad_gain_one = norm_backward(residual, gains[section, 0], grad_normed)
        grad_in = grad_middle + from_first
        grad_ins[section] = grad_in
        grad_out = grad_in.astype(bf16).astype(jnp.float32)
        spread = jnp.zeros((2, width), jnp.float32)
        spread = lax.dynamic_update_slice(
            spread, jnp.stack([grad_bound, grad_head_gain]), (0, place * local_width)
        )
        small[section] = jnp.concatenate([jnp.stack([grad_gain_one, grad_gain_two]), spread])
        shares[section] = [
            start_sum(part)
            for part in (grad_down, grad_pair_weight, grad_out_weight, grad_proj_weight)
        ]

    small_total = lax.psum(jnp.stack(small), ("pipe", "seq", "dp"))
    small_own = lax.dynamic_index_in_dim(small_total, core, 0, keepdims=False)
    local_small = lax.dynamic_slice(small_own, (2, place * local_width), (2, local_width))
    grad_down, grad_pair_weight, grad_out_weight, grad_proj_weight = [
        finish_sum(zero, one) for zero, one in zip(shares[0], shares[1])
    ]

    def exchange(zero, one):
        own = pick(first, zero, one)
        received = other_core(pick(first, one, zero))
        return jnp.stack([pick(first, own, received), pick(first, received, own)])[None, :, None]

    return (
        exchange(outs[0], outs[1]),
        exchange(grad_ins[0], grad_ins[1]),
        small_own[0][None],
        grad_proj_weight[:, :local_width][None],
        grad_proj_weight[:, local_width : 2 * local_width][None],
        grad_proj_weight[:, 2 * local_width :][None],
        local_small[0][None],
        local_small[1][None],
        grad_out_weight[None],
        small_own[1][None],
        grad_pair_weight[:, :hidden_here][None],
        grad_pair_weight[:, hidden_here:][None],
        grad_down[None],
    )


def solution(mesh):
    in_specs = (
        P(None, "dp", "seq", None),
        P(None, "dp", "seq", None),
        P(),
        P("pipe", None),
        P("pipe", None, "seq"),
        P("pipe", None, "seq"),
        P("pipe", None, "seq"),
        P("pipe", "seq"),
        P("pipe", "seq"),
        P("pipe", "seq", None),
        P("pipe", None),
        P("pipe", None, "seq"),
        P("pipe", None, "seq"),
        P("pipe", "seq", None),
    )
    out_specs = (
        P("pipe", None, "dp", "seq", None),
        P("pipe", None, "dp", "seq", None),
        P("pipe", None),
        P("pipe", None, "seq"),
        P("pipe", None, "seq"),
        P("pipe", None, "seq"),
        P("pipe", "seq"),
        P("pipe", "seq"),
        P("pipe", "seq", None),
        P("pipe", None),
        P("pipe", None, "seq"),
        P("pipe", None, "seq"),
        P("pipe", "seq", None),
    )
    return jax.shard_map(body, mesh=mesh, in_specs=in_specs, out_specs=out_specs, check_vma=False)
```

time: 4600 us -> 2140 us (0.47)
  other arithmetic: 1370 us -> 186 us
  matrix products: 842 us -> 270 us
  local copies, waits for them, and re-layouts: 582 us -> 109 us
  waiting for transfers between devices: 1610 us -> 1400 us
  blocking collectives: 140 us -> 3.8 us
  Pallas kernels: 0 us -> 67.6 us
  starting transfers between devices: 6.98 us -> 74.4 us
    reduce_sum x88 -> x10, other arithmetic: 859 us -> 22 us  [the longest x4 10.8 us: norm_backward(): grad_gain = jnp.sum(grad * unit, axis=0)]
    dot_general x90 -> x24, matrix products: 842 us -> 270 us  [dot(): lax.dot_general(left, right, (((left_dim,), (right_dim,)), ((), ())), pre...]
    ppermute x4 -> x74, waiting for transfers between devices: 7.65 us -> 419 us  [the longest x24 294 us: finish_sum(): lax.ppermute(piece, 'dp', pair_moves(step))]
    psum x1, waiting for transfers between devices: 364 us -> 107 us  [body(): small_total = lax.psum(jnp.stack(small), ('pipe', 'seq', 'dp'))]
    reduce_scatter x12 -> x8, waiting for transfers between devices: 541 us -> 330 us  [scatter_rows(): lax.psum_scatter(array, 'seq', scatter_dimension=0, tiled=True)]
    another operation x87 -> x4, local copies, waits for them, and re-layouts: 182 us -> 0.02 us
    add x147 -> x6, other arithmetic: 157 us -> 0.34 us  [small_sum(): total + lax.ppermute(array, axis, [(i, (i + step) % size) for i in range(...]
    all_gather x18 -> x12, waiting for transfers between devices: 694 us -> 542 us  [the longest x8 486 us: gather_rows(): return lax.all_gather(array, 'seq', axis=0, tiled=True)]
  transfers between devices with their start and end apart: 35 -> 95, of which waited for: 28 -> 52; matrix products, arithmetic and copies ran while one was open for 36% -> 21% of each run, Pallas kernels for 0% -> 2%
where the time goes in v1:
time: 2140 us; the launch traced here: 2120 us
  waiting for transfers between devices  1400 us (65%)
  matrix products  270 us (13%)
  other arithmetic  186 us (9%)
  local copies, waits for them, and re-layouts  109 us (5%)
  starting transfers between devices  74.4 us (3%)
  Pallas kernels  67.6 us (3%)
    all_gather x8, waiting for transfers between devices, gather_rows(): return lax.all_gather(array, 'seq', axis=0, tiled=True)  486 us
    reduce_scatter x8, waiting for transfers between devices, scatter_rows(): lax.psum_scatter(array, 'seq', scatter_dimension=0, tiled=True)  330 us
    ppermute x24, waiting for transfers between devices, finish_sum(): lax.ppermute(piece, 'dp', pair_moves(step))  294 us
    dot_general x24, matrix products, dot(): lax.dot_general(left, right, (((left_dim,), (right_dim,)), ((), ())), pre...  270 us
    psum x1, waiting for transfers between devices, body(): small_total = lax.psum(jnp.stack(small), ('pipe', 'seq', 'dp'))  107 us
    ppermute x24, waiting for transfers between devices, start_sum(): lax.ppermute(away, 'dp', pair_moves(step)).astype(jnp.float32)  101 us
    all_gather x4, waiting for transfers between devices, both(): return lax.all_gather(array, 'pipe', axis=0, tiled=False)  56.4 us
    dynamic_update_slice x32, other arithmetic, put(): lax.dynamic_update_slice(whole, piece.astype(jnp.float32)[None, None], (h...  45.9 us
  transfers between devices with their start and end apart: 95, of which 52 were waited for; matrix products, arithmetic and copies ran while one was open for 21% of the time, Pallas kernels for 2%

profile of v1, /device:TPU:0, one launch (start us, length us, event | category | flops | bytes accessed | tf_op | source)
XLA Modules:
  0.0 2124.8 jit_solution(11619392116418993623)
XLA Ops:
  29.9 67.6 %all-gather.17.cloned.1.call-done = bf16[1024,2048]{1,0:T(8,128)(2,1)} async-done(((bf16[256,2048]{1,0:T(8,128)(2,1)}), bf16[1024,2048]{1,0:T(8,128)(2,1)}) %all-gather.17.cloned.1.call-update) | async-done | bytes 4194320 | tf_op jit(solution)/shard_map/all_gather | solution.py:264
  97.5 25.3 %all-gather.19.cloned.1.call-done = bf16[2,2048,1536]{2,1,0:T(8,128)(2,1)} async-done(((bf16[1,2048,1536]{2,1,0:T(8,128)(2,1)}), bf16[2,2048,1536]{2,1,0:T(8,128)(2,1)}) %all-gather.19.cloned.1.call-update) | async-done | bytes 12582928 | tf_op jit(solution)/shard_map/all_gather | solution.py:343
  122.9 11.7 fusion.33.proj_ref
  134.6 15.3 rec_fwd.2
  150.0 6.3 convolution_convert_fusion.7
  161.2 8.2 convert.68
  169.3 7.8 pad_maximum_fusion
  187.8 46.8 %reduce-scatter.9.cloned.1.call-done = bf16[256,2048]{1,0:T(8,128)(2,1)} async-done(((bf16[1024,2048]{1,0:T(8,128)(2,1)}), bf16[256,2048]{1,0:T(8,128)(2,1)}) %reduce-scatter.9.cloned.1.call-update) | async-done | bytes 1048592 | tf_op jit(solution)/shard_map/reduce_scatter | solution.py:268
  239.2 9.9 convert_element_type.490
  249.6 25.3 %all-gather.25.cloned.1.call-done = bf16[2,2048,2816]{2,1,0:T(8,128)(2,1)} async-done(((bf16[1,2048,2816]{2,1,0:T(8,128)(2,1)}), bf16[2,2048,2816]{2,1,0:T(8,128)(2,1)}) %all-gather.25.cloned.1.call-update) | async-done | bytes 23068688 | tf_op jit(solution)/shard_map/all_gather | solution.py:343
  274.8 83.9 %all-gather.23.cloned.1.call-done = bf16[1024,2048]{1,0:T(8,128)(2,1)} async-done(((bf16[256,2048]{1,0:T(8,128)(2,1)}), bf16[1024,2048]{1,0:T(8,128)(2,1)}) %all-gather.23.cloned.1.call-update) | async-done | bytes 4194320 | tf_op jit(solution)/shard_map/all_gather | solution.py:264
  358.8 18.5 fusion.31
  383.1 12.4 fusion.43
  397.4 76.2 %reduce-scatter.11.cloned.1.call-done = bf16[256,2048]{1,0:T(8,128)(2,1)} async-done(((bf16[1024,2048]{1,0:T(8,128)(2,1)}), bf16[256,2048]{1,0:T(8,128)(2,1)}) %reduce-scatter.11.cloned.1.call-update) | async-done | bytes 1048592 | tf_op jit(solution)/shard_map/reduce_scatter | solution.py:268
  478.8 81.4 %all-gather.29.cloned.1.call-done = bf16[1024,2048]{1,0:T(8,128)(2,1)} async-done(((bf16[256,2048]{1,0:T(8,128)(2,1)}), bf16[1024,2048]{1,0:T(8,128)(2,1)}) %all-gather.29.cloned.1.call-update) | async-done | bytes 4194320 | tf_op jit(solution)/shard_map/all_gather | solution.py:264
  560.1 11.6 fusion.35.proj_ref
  571.8 15.2 rec_fwd.3
  587.0 6.3 convolution_convert_fusion.6
  600.6 68.2 %reduce-scatter.13.cloned.1.call-done = bf16[256,2048]{1,0:T(8,128)(2,1)} async-done(((bf16[1024,2048]{1,0:T(8,128)(2,1)}), bf16[256,2048]{1,0:T(8,128)(2,1)}) %reduce-scatter.13.cloned.1.call-update) | async-done | bytes 1048592 | tf_op jit(solution)/shard_map/reduce_scatter | solution.py:268
  674.1 80.6 %all-gather.31.cloned.1.call-done = bf16[1024,2048]{1,0:T(8,128)(2,1)} async-done(((bf16[256,2048]{1,0:T(8,128)(2,1)}), bf16[1024,2048]{1,0:T(8,128)(2,1)}) %all-gather.31.cloned.1.call-update) | async-done | bytes 4194320 | tf_op jit(solution)/shard_map/all_gather | solution.py:264
  754.7 18.5 fusion.30
  773.2 62.7 %all-gather.33.cloned.1.call-done = bf16[1024,2048]{1,0:T(8,128)(2,1)} async-done(((bf16[256,2048]{1,0:T(8,128)(2,1)}), bf16[1024,2048]{1,0:T(8,128)(2,1)}) %all-gather.33.cloned.1.call-update) | async-done | bytes 4194320 | tf_op jit(solution)/shard_map/all_gather | solution.py:264
  835.9 13.2 fusion.15
  851.7 16.3 fusion.40
  868.2 75.2 %reduce-scatter.17.cloned.1.call-done = bf16[256,2048]{1,0:T(8,128)(2,1)} async-done(((bf16[1024,2048]{1,0:T(8,128)(2,1)}), bf16[256,2048]{1,0:T(8,128)(2,1)}) %reduce-scatter.17.cloned.1.call-update) | async-done | bytes 1048592 | tf_op jit(solution)/shard_map/reduce_scatter | solution.py:268
  950.1 12.4 fusion.42
  972.6 59.2 %all-gather.35.cloned.1.call-done = bf16[1024,2048]{1,0:T(8,128)(2,1)} async-done(((bf16[256,2048]{1,0:T(8,128)(2,1)}), bf16[1024,2048]{1,0:T(8,128)(2,1)}) %all-gather.35.cloned.1.call-update) | async-done | bytes 4194320 | tf_op jit(solution)/shard_map/all_gather | solution.py:264
  1031.8 6.4 multiply_reduce_fusion
  1038.3 18.7 rec_bwd.2
  1056.9 11.1 fusion.44
  1068.5 18.3 convolution_convert_fusion
  1092.4 10.4 convolution_convert_fusion.2
  1126.2 63.7 %reduce-scatter.19.cloned.1.call-done = bf16[256,2048]{1,0:T(8,128)(2,1)} async-done(((bf16[1024,2048]{1,0:T(8,128)(2,1)}), bf16[256,2048]{1,0:T(8,128)(2,1)}) %reduce-scatter.19.cloned.1.call-update) | async-done | bytes 1048592 | tf_op jit(solution)/shard_map/reduce_scatter | solution.py:268
  1214.7 7.6 convolution_convert_fusion.4
  1227.6 50.1 %all-gather.37.cloned.1.call-done = bf16[1024,2048]{1,0:T(8,128)(2,1)} async-done(((bf16[256,2048]{1,0:T(8,128)(2,1)}), bf16[1024,2048]{1,0:T(8,128)(2,1)}) %all-gather.37.cloned.1.call-update) | async-done | bytes 4194320 | tf_op jit(solution)/shard_map/all_gather | solution.py:264
  1277.7 10.7 convolution_convert_fusion.3
  1293.3 13.8 fusion.11
  1307.1 16.2 convolution_convert_fusion.1
  1340.5 16.3 fusion.41
  1359.7 13.0 collective-permute-done.61
  1384.9 33.3 %collective-permute-done.67 = bf16[176,2048]{1,0:T(8,128)(2,1)S(1)} collective-permute-done((bf16[176,2048]{1,0:T(8,128)(2,1)S(1)}, bf16[176,2048]{1,0:T(8,128)(2,1)S(1)}, u32[]{:S(2)}, u32[]{:S(2)}) %collective-permute-start.67) | collective-permute-done | bytes 720928 | tf_op jit(solution)/shard_map/ppermute | solution.py:313
  1422.1 16.0 collective-permute-done.69
  1455.1 44.8 %collective-permute-done.72 = bf16[176,2048]{1,0:T(8,128)(2,1)} collective-permute-done((bf16[176,2048]{1,0:T(8,128)(2,1)S(1)}, bf16[176,2048]{1,0:T(8,128)(2,1)}, u32[]{:S(2)}, u32[]{:S(2)}) %collective-permute-start.72) | collective-permute-done | bytes 720928 | tf_op jit(solution)/shard_map/ppermute | solution.py:313
  1509.0 21.9 %collective-permute-done.47 = bf16[256,2816]{1,0:T(8,128)(2,1)S(1)} collective-permute-done((bf16[256,2816]{1,0:T(8,128)(2,1)S(1)}, bf16[256,2816]{1,0:T(8,128)(2,1)S(1)}, u32[]{:S(2)}, u32[]{:S(2)}) %collective-permute-start.47) | collective-permute-done | bytes 1441824 | tf_op jit(solution)/shard_map/ppermute | solution.py:291
  1530.9 29.2 %collective-permute-done.46 = bf16[256,2816]{1,0:T(8,128)(2,1)S(1)} collective-permute-done((bf16[256,2816]{1,0:T(8,128)(2,1)S(1)}, bf16[256,2816]{1,0:T(8,128)(2,1)S(1)}, u32[]{:S(2)}, u32[]{:S(2)}) %collective-permute-start.46) | collective-permute-done | bytes 1441824 | tf_op jit(solution)/shard_map/ppermute | solution.py:291
  1565.5 9.7 broadcast_in_dim.281
  1596.2 16.3 collective-permute-done.52
  1617.1 33.3 %collective-permute-done.53 = bf16[256,2816]{1,0:T(8,128)(2,1)} collective-permute-done((bf16[256,2816]{1,0:T(8,128)(2,1)}, bf16[256,2816]{1,0:T(8,128)(2,1)}, u32[]{:S(2)}, u32[]{:S(2)}) %collective-permute-start.53) | collective-permute-done | bytes 1441824 | tf_op jit(solution)/shard_map/ppermute | solution.py:313
  1661.2 25.8 %collective-permute-done.56 = bf16[256,2816]{1,0:T(8,128)(2,1)S(1)} collective-permute-done((bf16[256,2816]{1,0:T(8,128)(2,1)}, bf16[256,2816]{1,0:T(8,128)(2,1)S(1)}, u32[]{:S(2)}, u32[]{:S(2)}) %collective-permute-start.56) | collective-permute-done | bytes 1441824 | tf_op jit(solution)/shard_map/ppermute | solution.py:313
  1689.0 27.6 %collective-permute-done.57 = bf16[256,2816]{1,0:T(8,128)(2,1)S(1)} collective-permute-done((bf16[256,2816]{1,0:T(8,128)(2,1)}, bf16[256,2816]{1,0:T(8,128)(2,1)S(1)}, u32[]{:S(2)}, u32[]{:S(2)}) %collective-permute-start.57) | collective-permute-done | bytes 1441824 | tf_op jit(solution)/shard_map/ppermute | solution.py:313
  1720.1 17.1 slice_bitcast_fusion
  1747.0 18.3 rec_bwd.3
  1765.4 10.1 convolution_convert_fusion.5
  1800.0 11.0 fusion.45
  1817.2 20.2 collective-permute-done.38
  1848.0 16.3 collective-permute-done.41
  1869.4 12.6 collective-permute-done.17
  1883.5 14.4 collective-permute-done.15
  1915.1 13.4 collective-permute-done.22
  1931.2 16.6 collective-permute-done.23
  1951.8 10.4 collective-permute-done.26
  1963.6 17.4 collective-permute-done.27
  1992.5 9.9 slice_bitcast_fusion.24
  2002.5 107.1 %all-reduce.2.cloned.1.call-done = f32[2,4,2048]{2,1,0:T(4,128)} async-done(((f32[2,4,2048]{2,1,0:T(4,128)}), f32[2,4,2048]{2,1,0:T(4,128)}) %all-reduce.2.cloned.1.call-update) | async-done | bytes 65552 | tf_op jit(solution)/shard_map/psum | solution.py:445
  (470 shorter events, 364.2 us)
Async XLA Ops:
  7.2 90.4 %all-gather.17.cloned.1.call-start = ((), (), s32[]{:S(2)}) async-start(), calls=%async_computation.8 | async-start | bytes 5242880 | tf_op jit(solution)/shard_map/all_gather | solution.py:264
  14.1 108.8 %all-gather.19.cloned.1.call-start = ((), (), s32[]{:S(2)}) async-start(), calls=%async_computation.9 | async-start | bytes 18874368 | tf_op jit(solution)/shard_map/all_gather | solution.py:343
  23.1 126.9 %all-gather.21.cloned.1.call-start = ((), (), s32[]{:S(2)}) async-start(), calls=%async_computation.10 | async-start | bytes 6291456 | tf_op jit(solution)/shard_map/all_gather | solution.py:343
  27.4 207.2 %reduce-scatter.9.cloned.1.call-start = ((), (), s32[]{:S(2)}) async-start(), calls=%async_computation.11 | async-start | bytes 5242880 | tf_op jit(solution)/shard_map/reduce_scatter | solution.py:268
  156.3 118.6 %all-gather.25.cloned.1.call-start = ((), (), s32[]{:S(2)}) async-start(), calls=%async_computation.13 | async-start | bytes 34603008 | tf_op jit(solution)/shard_map/all_gather | solution.py:343
  177.2 181.6 %all-gather.23.cloned.1.call-start = ((), (), s32[]{:S(2)}) async-start(), calls=%async_computation.12 | async-start | bytes 5242880 | tf_op jit(solution)/shard_map/all_gather | solution.py:264
  239.2 143.9 %all-gather.27.cloned.1.call-start = ((), (), s32[]{:S(2)}) async-start(), calls=%async_computation.14 | async-start | bytes 17301504 | tf_op jit(solution)/shard_map/all_gather | solution.py:343
  249.2 224.4 %reduce-scatter.11.cloned.1.call-start = ((), (), s32[]{:S(2)}) async-start(), calls=%async_computation.15 | async-start | bytes 5242880 | tf_op jit(solution)/shard_map/reduce_scatter | solution.py:268
  395.5 164.6 %all-gather.29.cloned.1.call-start = ((), (), s32[]{:S(2)}) async-start(), calls=%async_computation.16 | async-start | bytes 5242880 | tf_op jit(solution)/shard_map/all_gather | solution.py:264
  478.7 190.1 %reduce-scatter.13.cloned.1.call-start = ((), (), s32[]{:S(2)}) async-start(), calls=%async_computation.17 | async-start | bytes 5242880 | tf_op jit(solution)/shard_map/reduce_scatter | solution.py:268
  593.3 161.4 %all-gather.31.cloned.1.call-start = ((), (), s32[]{:S(2)}) async-start(), calls=%async_computation.18 | async-start | bytes 5242880 | tf_op jit(solution)/shard_map/all_gather | solution.py:264
  673.3 162.6 %all-gather.33.cloned.1.call-start = ((), (), s32[]{:S(2)}) async-start(), calls=%async_computation.20 | async-start | bytes 5242880 | tf_op jit(solution)/shard_map/all_gather | solution.py:264
  673.9 269.5 %reduce-scatter.17.cloned.1.call-start = ((), (), s32[]{:S(2)}) async-start(), calls=%async_computation.21 | async-start | bytes 5242880 | tf_op jit(solution)/shard_map/reduce_scatter | solution.py:268
  868.0 163.9 %all-gather.35.cloned.1.call-start = ((), (), s32[]{:S(2)}) async-start(), calls=%async_computation.22 | async-start | bytes 5242880 | tf_op jit(solution)/shard_map/all_gather | solution.py:264
  950.1 173.2 %reduce-scatter.15.cloned.1.call-start = ((), (), s32[]{:S(2)}) async-start(), calls=%async_computation.19 | async-start | bytes 5242880 | tf_op jit(solution)/shard_map/reduce_scatter | solution.py:268
  962.5 227.3 %reduce-scatter.19.cloned.1.call-start = ((), (), s32[]{:S(2)}) async-start(), calls=%async_computation.23 | async-start | bytes 5242880 | tf_op jit(solution)/shard_map/reduce_scatter | solution.py:268
  1068.0 209.7 %all-gather.37.cloned.1.call-start = ((), (), s32[]{:S(2)}) async-start(), calls=%async_computation.24 | async-start | bytes 5242880 | tf_op jit(solution)/shard_map/all_gather | solution.py:264
  1092.4 104.0 %collective-permute-start.48 = (bf16[1024,2816]{1,0:T(8,128)(2,1)}, bf16[1024,2816]{1,0:T(8,128)(2,1)}, u32[]{:S(2)}, u32[]{:S(2)}) collective-permute-start(bf16[1024,2816]{1,0:T(8,128)(2,1)} %dynamic-slice_bitcast_fusion), channel_id=1, source_target_pairs={{0,16},{16,0},{1,17},{17,1},{2,18},{18,2},{3,19},{19,3},{4,20},{20... | collective-permute-start | bytes 17301512 | tf_op jit(solution)/shard_map/ppermute | solution.py:228
  1119.8 217.3 %collective-permute-start.66 = (bf16[176,2048]{1,0:T(8,128)(2,1)}, bf16[176,2048]{1,0:T(8,128)(2,1)}, u32[]{:S(2)}, u32[]{:S(2)}) collective-permute-start(bf16[176,2048]{1,0:T(8,128)(2,1)} %get-tuple-element.130), channel_id=1, source_target_pairs={{0,3},{1,2},{2,1},{3,0},{4,7},{5,6},{6,5},{7,4},{8,11},{9,10},{10,... | collective-permute-start | bytes 2162696 | tf_op jit(solution)/shard_map/ppermute | solution.py:291
  1122.0 217.4 %collective-permute-start.65 = (bf16[176,2048]{1,0:T(8,128)(2,1)}, bf16[176,2048]{1,0:T(8,128)(2,1)}, u32[]{:S(2)}, u32[]{:S(2)}) collective-permute-start(bf16[176,2048]{1,0:T(8,128)(2,1)} %get-tuple-element.131), channel_id=1, source_target_pairs={{0,2},{1,3},{2,0},{3,1},{4,6},{5,7},{6,4},{7,5},{8,10},{9,11},{10,... | collective-permute-start | bytes 2162696 | tf_op jit(solution)/shard_map/ppermute | solution.py:291
  1122.6 217.4 %collective-permute-start.64 = (bf16[176,2048]{1,0:T(8,128)(2,1)}, bf16[176,2048]{1,0:T(8,128)(2,1)}, u32[]{:S(2)}, u32[]{:S(2)}) collective-permute-start(bf16[176,2048]{1,0:T(8,128)(2,1)} %get-tuple-element.129), channel_id=1, source_target_pairs={{0,1},{1,0},{2,3},{3,2},{4,5},{5,4},{6,7},{7,6},{8,9},{9,8},{10,11... | collective-permute-start | bytes 2162696 | tf_op jit(solution)/shard_map/ppermute | solution.py:291
  1126.2 79.7 %collective-permute-start.6 = (bf16[256,2048]{1,0:T(8,128)(2,1)}, bf16[256,2048]{1,0:T(8,128)(2,1)}, u32[]{:S(2)}, u32[]{:S(2)}) collective-permute-start(bf16[256,2048]{1,0:T(8,128)(2,1)} %broadcast_select_fusion.4), channel_id=1, source_target_pairs={{0,16},{16,0},{1,17},{17,1},{2,18},{18,2},{3,19},{19,3},{4,20},{20... | collective-permute-start | bytes 3145736 | tf_op jit(solution)/shard_map/ppermute | solution.py:228
  1196.3 383.5 %reduce-scatter.21.cloned.1.call-start = ((), (), s32[]{:S(2)}) async-start(), calls=%async_computation.25 | async-start | bytes 5242880 | tf_op jit(solution)/shard_map/reduce_scatter | solution.py:268
  1226.0 154.0 %collective-permute-start.18 = (bf16[1024,1536]{1,0:T(8,128)(2,1)}, bf16[1024,1536]{1,0:T(8,128)(2,1)}, u32[]{:S(2)}, u32[]{:S(2)}) collective-permute-start(bf16[1024,1536]{1,0:T(8,128)(2,1)} %dynamic-slice_bitcast_fusion.2), channel_id=1, source_target_pairs={{0,16},{16,0},{1,17},{17,1},{2,18},{18,2},{3,19},{19,3},{4,20},{20... | collective-permute-start | bytes 9437192 | tf_op jit(solution)/shard_map/ppermute | solution.py:228
  1293.2 37.7 %collective-permute-start.59 = (bf16[704,2048]{1,0:T(8,128)(2,1)}, bf16[704,2048]{1,0:T(8,128)(2,1)}, u32[]{:S(2)}, u32[]{:S(2)}) collective-permute-start(bf16[704,2048]{1,0:T(8,128)(2,1)} %dynamic-slice_bitcast_fusion.5), channel_id=1, source_target_pairs={{0,16},{16,0},{1,17},{17,1},{2,18},{18,2},{3,19},{19,3},{4,20},{20... | collective-permute-start | bytes 8650760 | tf_op jit(solution)/shard_map/ppermute | solution.py:228
  1330.9 108.1 %collective-permute-start.44 = (bf16[1024,2816]{1,0:T(8,128)(2,1)}, bf16[1024,2816]{1,0:T(8,128)(2,1)}, u32[]{:S(2)}, u32[]{:S(2)}) collective-permute-start(bf16[1024,2816]{1,0:T(8,128)(2,1)} %dynamic-slice_bitcast_fusion.1), channel_id=1, source_target_pairs={{0,16},{16,0},{1,17},{17,1},{2,18},{18,2},{3,19},{19,3},{4,20},{20... | collective-permute-start | bytes 17301512 | tf_op jit(solution)/shard_map/ppermute | solution.py:228
  1339.4 33.3 %collective-permute-start.61 = (bf16[176,2048]{1,0:T(8,128)(2,1)S(1)}, bf16[176,2048]{1,0:T(8,128)(2,1)}, u32[]{:S(2)}, u32[]{:S(2)}) collective-permute-start(bf16[176,2048]{1,0:T(8,128)(2,1)S(1)} %get-tuple-element.128), channel_id=1, source_target_pairs={{0,2},{1,3},{2,0},{3,1},{4,6},{5,7},{6,4},{7,5},{8,10},{9,11},{10,... | collective-permute-start | bytes 2162696 | tf_op jit(solution)/shard_map/ppermute | solution.py:291
  1356.8 380.4 %all-gather.39.cloned.1.call-start = ((), (), s32[]{:S(2)}) async-start(), calls=%async_computation.26 | async-start | bytes 5242880 | tf_op jit(solution)/shard_map/all_gather | solution.py:264
  1357.3 94.5 %collective-permute-start.51 = (bf16[256,2816]{1,0:T(8,128)(2,1)}, bf16[256,2816]{1,0:T(8,128)(2,1)}, u32[]{:S(2)}, u32[]{:S(2)}) collective-permute-start(bf16[256,2816]{1,0:T(8,128)(2,1)} %get-tuple-element.112), channel_id=1, source_target_pairs={{0,3},{1,2},{2,1},{3,0},{4,7},{5,6},{6,5},{7,4},{8,11},{9,10},{10,... | collective-permute-start | bytes 4325384 | tf_op jit(solution)/shard_map/ppermute | solution.py:291
  1378.5 39.6 %collective-permute-start.67 = (bf16[176,2048]{1,0:T(8,128)(2,1)S(1)}, bf16[176,2048]{1,0:T(8,128)(2,1)S(1)}, u32[]{:S(2)}, u32[]{:S(2)}) collective-permute-start(bf16[176,2048]{1,0:T(8,128)(2,1)S(1)} %get-tuple-element.71), channel_id=1, source_target_pairs={{0,1},{1,0},{2,3},{3,2},{4,5},{5,4},{6,7},{7,6},{8,9},{9,8},{10,11... | collective-permute-start | bytes 2162696 | tf_op jit(solution)/shard_map/ppermute | solution.py:313
  1382.8 37.0 %collective-permute-start.68 = (bf16[176,2048]{1,0:T(8,128)(2,1)S(1)}, bf16[176,2048]{1,0:T(8,128)(2,1)S(1)}, u32[]{:S(2)}, u32[]{:S(2)}) collective-permute-start(bf16[176,2048]{1,0:T(8,128)(2,1)S(1)} %get-tuple-element.71), channel_id=1, source_target_pairs={{0,2},{1,3},{2,0},{3,1},{4,6},{5,7},{6,4},{7,5},{8,10},{9,11},{10,... | collective-permute-start | bytes 2162696 | tf_op jit(solution)/shard_map/ppermute | solution.py:313
  1383.4 37.9 %collective-permute-start.70 = (bf16[176,2048]{1,0:T(8,128)(2,1)S(1)}, bf16[176,2048]{1,0:T(8,128)(2,1)S(1)}, u32[]{:S(2)}, u32[]{:S(2)}) collective-permute-start(bf16[176,2048]{1,0:T(8,128)(2,1)S(1)} %get-tuple-element.67), channel_id=1, source_target_pairs={{0,16},{16,0},{1,17},{17,1},{2,18},{18,2},{3,19},{19,3},{4,20},{20... | collective-permute-start | bytes 2162696 | tf_op jit(solution)/shard_map/ppermute | solution.py:228
  1419.8 89.2 %collective-permute-start.50 = (bf16[256,2816]{1,0:T(8,128)(2,1)S(1)}, bf16[256,2816]{1,0:T(8,128)(2,1)}, u32[]{:S(2)}, u32[]{:S(2)}) collective-permute-start(bf16[256,2816]{1,0:T(8,128)(2,1)S(1)} %copy-done.32), channel_id=1, source_target_pairs={{0,2},{1,3},{2,0},{3,1},{4,6},{5,7},{6,4},{7,5},{8,10},{9,11},{10,... | collective-permute-start | bytes 4325384 | tf_op jit(solution)/shard_map/ppermute | solution.py:291
  1438.1 61.8 %collective-permute-start.72 = (bf16[176,2048]{1,0:T(8,128)(2,1)S(1)}, bf16[176,2048]{1,0:T(8,128)(2,1)}, u32[]{:S(2)}, u32[]{:S(2)}) collective-permute-start(bf16[176,2048]{1,0:T(8,128)(2,1)S(1)} %collective-permute-done.70), channel_id=1, source_target_pairs={{0,2},{1,3},{2,0},{3,1},{4,6},{5,7},{6,4},{7,5},{8,10},{9,11},{10,... | collective-permute-start | bytes 2162696 | tf_op jit(solution)/shard_map/ppermute | solution.py:313
  1443.4 57.0 %collective-permute-start.73 = (bf16[176,2048]{1,0:T(8,128)(2,1)S(1)}, bf16[176,2048]{1,0:T(8,128)(2,1)}, u32[]{:S(2)}, u32[]{:S(2)}) collective-permute-start(bf16[176,2048]{1,0:T(8,128)(2,1)S(1)} %collective-permute-done.70), channel_id=1, source_target_pairs={{0,3},{1,2},{2,1},{3,0},{4,7},{5,6},{6,5},{7,4},{8,11},{9,10},{10,... | collective-permute-start | bytes 2162696 | tf_op jit(solution)/shard_map/ppermute | solution.py:313
  1451.8 57.2 %collective-permute-start.49 = (bf16[256,2816]{1,0:T(8,128)(2,1)S(1)}, bf16[256,2816]{1,0:T(8,128)(2,1)S(1)}, u32[]{:S(2)}, u32[]{:S(2)}) collective-permute-start(bf16[256,2816]{1,0:T(8,128)(2,1)S(1)} %get-tuple-element.111), channel_id=1, source_target_pairs={{0,1},{1,0},{2,3},{3,2},{4,5},{5,4},{6,7},{7,6},{8,9},{9,8},{10,11... | collective-permute-start | bytes 4325384 | tf_op jit(solution)/shard_map/ppermute | solution.py:291
  1452.8 78.1 %collective-permute-start.47 = (bf16[256,2816]{1,0:T(8,128)(2,1)S(1)}, bf16[256,2816]{1,0:T(8,128)(2,1)S(1)}, u32[]{:S(2)}, u32[]{:S(2)}) collective-permute-start(bf16[256,2816]{1,0:T(8,128)(2,1)S(1)} %get-tuple-element.109), channel_id=1, source_target_pairs={{0,3},{1,2},{2,1},{3,0},{4,7},{5,6},{6,5},{7,4},{8,11},{9,10},{10,... | collective-permute-start | bytes 4325384 | tf_op jit(solution)/shard_map/ppermute | solution.py:291
  1499.9 60.2 %collective-permute-start.46 = (bf16[256,2816]{1,0:T(8,128)(2,1)S(1)}, bf16[256,2816]{1,0:T(8,128)(2,1)S(1)}, u32[]{:S(2)}, u32[]{:S(2)}) collective-permute-start(bf16[256,2816]{1,0:T(8,128)(2,1)S(1)} %get-tuple-element.110), channel_id=1, source_target_pairs={{0,2},{1,3},{2,0},{3,1},{4,6},{5,7},{6,4},{7,5},{8,10},{9,11},{10,... | collective-permute-start | bytes 4325384 | tf_op jit(solution)/shard_map/ppermute | solution.py:291
  1500.4 59.7 %collective-permute-start.45 = (bf16[256,2816]{1,0:T(8,128)(2,1)S(1)}, bf16[256,2816]{1,0:T(8,128)(2,1)S(1)}, u32[]{:S(2)}, u32[]{:S(2)}) collective-permute-start(bf16[256,2816]{1,0:T(8,128)(2,1)S(1)} %get-tuple-element.108), channel_id=1, source_target_pairs={{0,1},{1,0},{2,3},{3,2},{4,5},{5,4},{6,7},{7,6},{8,9},{9,8},{10,11... | collective-permute-start | bytes 4325384 | tf_op jit(solution)/shard_map/ppermute | solution.py:291
  1577.7 34.8 %collective-permute-start.52 = (bf16[256,2816]{1,0:T(8,128)(2,1)}, bf16[256,2816]{1,0:T(8,128)(2,1)}, u32[]{:S(2)}, u32[]{:S(2)}) collective-permute-start(bf16[256,2816]{1,0:T(8,128)(2,1)} %get-tuple-element.76), channel_id=1, source_target_pairs={{0,1},{1,0},{2,3},{3,2},{4,5},{5,4},{6,7},{7,6},{8,9},{9,8},{10,11... | collective-permute-start | bytes 4325384 | tf_op jit(solution)/shard_map/ppermute | solution.py:313
  1579.2 71.3 %collective-permute-start.53 = (bf16[256,2816]{1,0:T(8,128)(2,1)}, bf16[256,2816]{1,0:T(8,128)(2,1)}, u32[]{:S(2)}, u32[]{:S(2)}) collective-permute-start(bf16[256,2816]{1,0:T(8,128)(2,1)} %get-tuple-element.76), channel_id=1, source_target_pairs={{0,2},{1,3},{2,0},{3,1},{4,6},{5,7},{6,4},{7,5},{8,10},{9,11},{10,... | collective-permute-start | bytes 4325384 | tf_op jit(solution)/shard_map/ppermute | solution.py:313
  1579.8 71.2 %collective-permute-start.55 = (bf16[256,2816]{1,0:T(8,128)(2,1)}, bf16[256,2816]{1,0:T(8,128)(2,1)}, u32[]{:S(2)}, u32[]{:S(2)}) collective-permute-start(bf16[256,2816]{1,0:T(8,128)(2,1)} %get-tuple-element.72), channel_id=1, source_target_pairs={{0,16},{16,0},{1,17},{17,1},{2,18},{18,2},{3,19},{19,3},{4,20},{20... | collective-permute-start | bytes 4325384 | tf_op jit(solution)/shard_map/ppermute | solution.py:228
  1587.2 395.2 %reduce-scatter.23.cloned.1.call-start = ((), (), s32[]{:S(2)}) async-start(), calls=%async_computation.27 | async-start | bytes 5242880 | tf_op jit(solution)/shard_map/reduce_scatter | solution.py:268
  1590.4 189.7 %collective-permute-start.36 = (bf16[64,2048]{1,0:T(8,128)(2,1)}, bf16[64,2048]{1,0:T(8,128)(2,1)}, u32[]{:S(2)}, u32[]{:S(2)}) collective-permute-start(bf16[64,2048]{1,0:T(8,128)(2,1)} %get-tuple-element.136), channel_id=1, source_target_pairs={{0,3},{1,2},{2,1},{3,0},{4,7},{5,6},{6,5},{7,4},{8,11},{9,10},{10,... | collective-permute-start | bytes 786440 | tf_op jit(solution)/shard_map/ppermute | solution.py:291
  1594.7 188.7 %collective-permute-start.35 = (bf16[64,2048]{1,0:T(8,128)(2,1)}, bf16[64,2048]{1,0:T(8,128)(2,1)}, u32[]{:S(2)}, u32[]{:S(2)}) collective-permute-start(bf16[64,2048]{1,0:T(8,128)(2,1)} %get-tuple-element.137), channel_id=1, source_target_pairs={{0,2},{1,3},{2,0},{3,1},{4,6},{5,7},{6,4},{7,5},{8,10},{9,11},{10,... | collective-permute-start | bytes 786440 | tf_op jit(solution)/shard_map/ppermute | solution.py:291
  1612.5 43.2 %collective-permute-start.54 = (bf16[256,2816]{1,0:T(8,128)(2,1)}, bf16[256,2816]{1,0:T(8,128)(2,1)S(1)}, u32[]{:S(2)}, u32[]{:S(2)}) collective-permute-start(bf16[256,2816]{1,0:T(8,128)(2,1)} %get-tuple-element.76), channel_id=1, source_target_pairs={{0,3},{1,2},{2,1},{3,0},{4,7},{5,6},{6,5},{7,4},{8,11},{9,10},{10,... | collective-permute-start | bytes 4325384 | tf_op jit(solution)/shard_map/ppermute | solution.py:313
  1650.5 133.0 %collective-permute-start.34 = (bf16[64,2048]{1,0:T(8,128)(2,1)S(1)}, bf16[64,2048]{1,0:T(8,128)(2,1)}, u32[]{:S(2)}, u32[]{:S(2)}) collective-permute-start(bf16[64,2048]{1,0:T(8,128)(2,1)S(1)} %copy-done.34), channel_id=1, source_target_pairs={{0,1},{1,0},{2,3},{3,2},{4,5},{5,4},{6,7},{7,6},{8,9},{9,8},{10,11... | collective-permute-start | bytes 786440 | tf_op jit(solution)/shard_map/ppermute | solution.py:291
  1651.0 35.9 %collective-permute-start.56 = (bf16[256,2816]{1,0:T(8,128)(2,1)}, bf16[256,2816]{1,0:T(8,128)(2,1)S(1)}, u32[]{:S(2)}, u32[]{:S(2)}) collective-permute-start(bf16[256,2816]{1,0:T(8,128)(2,1)} %collective-permute-done.55), channel_id=1, source_target_pairs={{0,1},{1,0},{2,3},{3,2},{4,5},{5,4},{6,7},{7,6},{8,9},{9,8},{10,11... | collective-permute-start | bytes 4325384 | tf_op jit(solution)/shard_map/ppermute | solution.py:313
  1655.7 60.8 %collective-permute-start.57 = (bf16[256,2816]{1,0:T(8,128)(2,1)}, bf16[256,2816]{1,0:T(8,128)(2,1)S(1)}, u32[]{:S(2)}, u32[]{:S(2)}) collective-permute-start(bf16[256,2816]{1,0:T(8,128)(2,1)} %collective-permute-done.55), channel_id=1, source_target_pairs={{0,2},{1,3},{2,0},{3,1},{4,6},{5,7},{6,4},{7,5},{8,10},{9,11},{10,... | collective-permute-start | bytes 4325384 | tf_op jit(solution)/shard_map/ppermute | solution.py:313
  1783.4 63.2 %collective-permute-start.21 = (bf16[256,1536]{1,0:T(8,128)(2,1)}, bf16[256,1536]{1,0:T(8,128)(2,1)}, u32[]{:S(2)}, u32[]{:S(2)}) collective-permute-start(bf16[256,1536]{1,0:T(8,128)(2,1)} %get-tuple-element.124), channel_id=1, source_target_pairs={{0,3},{1,2},{2,1},{3,0},{4,7},{5,6},{6,5},{7,4},{8,11},{9,10},{10,... | collective-permute-start | bytes 2359304 | tf_op jit(solution)/shard_map/ppermute | solution.py:291
  1783.5 83.9 %collective-permute-start.20 = (bf16[256,1536]{1,0:T(8,128)(2,1)}, bf16[256,1536]{1,0:T(8,128)(2,1)}, u32[]{:S(2)}, u32[]{:S(2)}) collective-permute-start(bf16[256,1536]{1,0:T(8,128)(2,1)} %get-tuple-element.125), channel_id=1, source_target_pairs={{0,2},{1,3},{2,0},{3,1},{4,6},{5,7},{6,4},{7,5},{8,10},{9,11},{10,... | collective-permute-start | bytes 2359304 | tf_op jit(solution)/shard_map/ppermute | solution.py:291
  1788.2 53.1 %collective-permute-start.14 = (bf16[1024,1536]{1,0:T(8,128)(2,1)}, bf16[1024,1536]{1,0:T(8,128)(2,1)}, u32[]{:S(2)}, u32[]{:S(2)}) collective-permute-start(bf16[1024,1536]{1,0:T(8,128)(2,1)} %dynamic-slice_bitcast_fusion.3), channel_id=1, source_target_pairs={{0,16},{16,0},{1,17},{17,1},{2,18},{18,2},{3,19},{19,3},{4,20},{20... | collective-permute-start | bytes 9437192 | tf_op jit(solution)/shard_map/ppermute | solution.py:228
  1811.1 298.5 %all-reduce.2.cloned.1.call-start = ((), (), s32[]{:S(2)}) async-start(), calls=%async_computation.28 | async-start | bytes 131072 | tf_op jit(solution)/shard_map/psum | solution.py:445
  1845.2 36.7 %collective-permute-start.17 = (bf16[256,1536]{1,0:T(8,128)(2,1)S(1)}, bf16[256,1536]{1,0:T(8,128)(2,1)S(1)}, u32[]{:S(2)}, u32[]{:S(2)}) collective-permute-start(bf16[256,1536]{1,0:T(8,128)(2,1)S(1)} %get-tuple-element.121), channel_id=1, source_target_pairs={{0,3},{1,2},{2,1},{3,0},{4,7},{5,6},{6,5},{7,4},{8,11},{9,10},{10,... | collective-permute-start | bytes 2359304 | tf_op jit(solution)/shard_map/ppermute | solution.py:291
  1846.6 36.9 %collective-permute-start.16 = (bf16[256,1536]{1,0:T(8,128)(2,1)S(1)}, bf16[256,1536]{1,0:T(8,128)(2,1)S(1)}, u32[]{:S(2)}, u32[]{:S(2)}) collective-permute-start(bf16[256,1536]{1,0:T(8,128)(2,1)S(1)} %get-tuple-element.122), channel_id=1, source_target_pairs={{0,2},{1,3},{2,0},{3,1},{4,6},{5,7},{6,4},{7,5},{8,10},{9,11},{10,... | collective-permute-start | bytes 2359304 | tf_op jit(solution)/shard_map/ppermute | solution.py:291
  1864.2 33.8 %collective-permute-start.15 = (bf16[256,1536]{1,0:T(8,128)(2,1)S(1)}, bf16[256,1536]{1,0:T(8,128)(2,1)S(1)}, u32[]{:S(2)}, u32[]{:S(2)}) collective-permute-start(bf16[256,1536]{1,0:T(8,128)(2,1)S(1)} %get-tuple-element.120), channel_id=1, source_target_pairs={{0,1},{1,0},{2,3},{3,2},{4,5},{5,4},{6,7},{7,6},{8,9},{9,8},{10,11... | collective-permute-start | bytes 2359304 | tf_op jit(solution)/shard_map/ppermute | solution.py:291
  1867.4 42.2 %collective-permute-start.42 = (bf16[64,2048]{1,0:T(8,128)(2,1)S(1)}, bf16[64,2048]{1,0:T(8,128)(2,1)S(1)}, u32[]{:S(2)}, u32[]{:S(2)}) collective-permute-start(bf16[64,2048]{1,0:T(8,128)(2,1)S(1)} %collective-permute-done.40), channel_id=1, source_target_pairs={{0,2},{1,3},{2,0},{3,1},{4,6},{5,7},{6,4},{7,5},{8,10},{9,11},{10,... | collective-permute-start | bytes 786440 | tf_op jit(solution)/shard_map/ppermute | solution.py:313
  1867.7 43.1 %collective-permute-start.43 = (bf16[64,2048]{1,0:T(8,128)(2,1)S(1)}, bf16[64,2048]{1,0:T(8,128)(2,1)S(1)}, u32[]{:S(2)}, u32[]{:S(2)}) collective-permute-start(bf16[64,2048]{1,0:T(8,128)(2,1)S(1)} %collective-permute-done.40), channel_id=1, source_target_pairs={{0,3},{1,2},{2,1},{3,0},{4,7},{5,6},{6,5},{7,4},{8,11},{9,10},{10,... | collective-permute-start | bytes 786440 | tf_op jit(solution)/shard_map/ppermute | solution.py:313
  1910.5 37.3 %collective-permute-start.23 = (bf16[256,1536]{1,0:T(8,128)(2,1)S(1)}, bf16[256,1536]{1,0:T(8,128)(2,1)S(1)}, u32[]{:S(2)}, u32[]{:S(2)}) collective-permute-start(bf16[256,1536]{1,0:T(8,128)(2,1)S(1)} %get-tuple-element.86), channel_id=1, source_target_pairs={{0,2},{1,3},{2,0},{3,1},{4,6},{5,7},{6,4},{7,5},{8,10},{9,11},{10,... | collective-permute-start | bytes 2359304 | tf_op jit(solution)/shard_map/ppermute | solution.py:313
  1911.6 37.4 %collective-permute-start.24 = (bf16[256,1536]{1,0:T(8,128)(2,1)S(1)}, bf16[256,1536]{1,0:T(8,128)(2,1)S(1)}, u32[]{:S(2)}, u32[]{:S(2)}) collective-permute-start(bf16[256,1536]{1,0:T(8,128)(2,1)S(1)} %get-tuple-element.86), channel_id=1, source_target_pairs={{0,3},{1,2},{2,1},{3,0},{4,7},{5,6},{6,5},{7,4},{8,11},{9,10},{10,... | collective-permute-start | bytes 2359304 | tf_op jit(solution)/shard_map/ppermute | solution.py:313
  1913.2 49.0 %collective-permute-start.26 = (bf16[256,1536]{1,0:T(8,128)(2,1)S(1)}, bf16[256,1536]{1,0:T(8,128)(2,1)S(1)}, u32[]{:S(2)}, u32[]{:S(2)}) collective-permute-start(bf16[256,1536]{1,0:T(8,128)(2,1)S(1)} %collective-permute-done.25), channel_id=1, source_target_pairs={{0,1},{1,0},{2,3},{3,2},{4,5},{5,4},{6,7},{7,6},{8,9},{9,8},{10,11... | collective-permute-start | bytes 2359304 | tf_op jit(solution)/shard_map/ppermute | solution.py:313
  1914.8 66.2 %collective-permute-start.27 = (bf16[256,1536]{1,0:T(8,128)(2,1)S(1)}, bf16[256,1536]{1,0:T(8,128)(2,1)S(1)}, u32[]{:S(2)}, u32[]{:S(2)}) collective-permute-start(bf16[256,1536]{1,0:T(8,128)(2,1)S(1)} %collective-permute-done.25), channel_id=1, source_target_pairs={{0,2},{1,3},{2,0},{3,1},{4,6},{5,7},{6,4},{7,5},{8,10},{9,11},{10,... | collective-permute-start | bytes 2359304 | tf_op jit(solution)/shard_map/ppermute | solution.py:313
  1928.5 60.8 %collective-permute-start.28 = (bf16[256,1536]{1,0:T(8,128)(2,1)S(1)}, bf16[256,1536]{1,0:T(8,128)(2,1)}, u32[]{:S(2)}, u32[]{:S(2)}) collective-permute-start(bf16[256,1536]{1,0:T(8,128)(2,1)S(1)} %collective-permute-done.25), channel_id=1, source_target_pairs={{0,3},{1,2},{2,1},{3,0},{4,7},{5,6},{6,5},{7,4},{8,11},{9,10},{10,... | collective-permute-start | bytes 2359304 | tf_op jit(solution)/shard_map/ppermute | solution.py:313
  1989.3 123.1 %collective-permute-start.13 = (f32[256,2048]{1,0:T(8,128)}, f32[256,2048]{1,0:T(8,128)}, u32[]{:S(2)}, u32[]{:S(2)}) collective-permute-start(f32[256,2048]{1,0:T(8,128)} %get-tuple-element.87), channel_id=1, source_target_pairs={{0,16},{16,0},{1,17},{17,1},{2,18},{18,2},{3,19},{19,3},{4,20},{20... | collective-permute-start | bytes 6291464 | tf_op jit(solution)/shard_map/ppermute | solution.py:228
  (109 other events, 2664.2 us)
Sparse Core Ops, SparseCore 0:
  14.2 83.3 all-gather.16
  99.7 23.1 all-gather.18
  125.0 14.8 all-gather.20
  156.4 78.2 reduce-scatter.8
  236.6 38.1 all-gather.24
  276.8 81.9 all-gather.22
  360.9 22.1 all-gather.26
  395.6 77.9 reduce-scatter.10
  478.8 81.2 all-gather.28
  593.4 75.3 reduce-scatter.12
  673.4 81.1 all-gather.30
  756.7 79.2 all-gather.32
  868.1 75.2 reduce-scatter.16
  950.2 81.6 all-gather.34
  1034.5 75.1 reduce-scatter.14
  1112.5 77.2 reduce-scatter.18
  1196.4 81.2 all-gather.36
  1356.9 75.2 reduce-scatter.20
  1587.4 79.9 all-gather.38
  1811.2 74.3 reduce-scatter.22
  1992.6 116.8 all-reduce.1

commit v2 on v1

--- a/solution.py
+++ b/solution.py
@@ -1,3 +1,5 @@
+import functools
+
 import jax
 import jax.numpy as jnp
 from jax import lax
@@ -6,6 +8,8 @@
 from jax.sharding import PartitionSpec as P
 
 EPSILON = 1e-06
+PIECES = 16
+LAG = 2
 SPAN = 128
 HEAD = 128
 HIGH = lax.Precision.HIGHEST
@@ -224,6 +228,237 @@
     return dproj, glb[0]
 
 
+def neighbour_barrier(place, count, right, left):
+    barrier = pltpu.get_barrier_semaphore()
+
+    @pl.when(place > 0)
+    def _():
+        pl.semaphore_signal(
+            barrier, inc=1, device_id={"seq": left}, device_id_type=pl.DeviceIdType.MESH
+        )
+
+    @pl.when(place < count - 1)
+    def _():
+        pl.semaphore_signal(
+            barrier, inc=1, device_id={"seq": right}, device_id_type=pl.DeviceIdType.MESH
+        )
+
+    inner = jnp.logical_and(place > 0, place < count - 1)
+
+    @pl.when(inner)
+    def _():
+        pl.semaphore_wait(barrier, 2)
+
+    @pl.when(jnp.logical_not(inner))
+    def _():
+        pl.semaphore_wait(barrier, 1)
+
+
+def send(source, target, send_sem, recv_sem, device):
+    return pltpu.make_async_remote_copy(
+        src_ref=source,
+        dst_ref=target,
+        send_sem=send_sem,
+        recv_sem=recv_sem,
+        device_id={"seq": device},
+        device_id_type=pl.DeviceIdType.MESH,
+    )
+
+
+def each(count, step):
+    def run(i, carry):
+        step(i)
+        return carry
+
+    lax.fori_loop(0, count, run, 0)
+
+
+def relay(place, count, pass_right, pass_left, finish):
+    def run(early, late):
+        def step(i):
+            @pl.when(i < PIECES)
+            def _():
+                early(i)
+
+            @pl.when(i >= LAG)
+            def _():
+                late(i - LAG)
+
+        each(PIECES + LAG, step)
+        each(PIECES, finish)
+
+    @pl.when(jnp.logical_and(place > 0, place < count // 2))
+    def _():
+        run(pass_right, pass_left)
+
+    @pl.when(jnp.logical_and(place >= count // 2, place < count - 1))
+    def _():
+        run(pass_left, pass_right)
+
+
+def line_gather_kernel(count, x_ref, out_ref, send_right, recv_right, send_left, recv_left, own_sem):
+    place = lax.axis_index("seq")
+    right, left = lax.rem(place + 1, count), lax.rem(place + count - 1, count)
+    half = x_ref.shape[0]
+    rows = half // PIECES
+    neighbour_barrier(place, count, right, left)
+
+    def low(i):
+        return out_ref.at[pl.ds(pl.multiple_of(i * rows, rows), rows)]
+
+    def high(i):
+        return out_ref.at[pl.ds(pl.multiple_of(half + i * rows, rows), rows)]
+
+    def own(i):
+        return x_ref.at[pl.ds(pl.multiple_of(i * rows, rows), rows)]
+
+    def rightward(i, source):
+        return send(source, low(i), send_right.at[i], recv_right.at[i], right)
+
+    def leftward(i, source):
+        return send(source, high(i), send_left.at[i], recv_left.at[i], left)
+
+    @pl.when(place == 0)
+    def _():
+        each(PIECES, lambda i: rightward(i, own(i)).start())
+        keep = pltpu.make_async_copy(x_ref, out_ref.at[pl.ds(0, half)], own_sem)
+        keep.start()
+        each(PIECES, lambda i: leftward(i, high(i)).wait_recv())
+        keep.wait()
+        each(PIECES, lambda i: rightward(i, own(i)).wait_send())
+
+    @pl.when(place == count - 1)
+    def _():
+        each(PIECES, lambda i: leftward(i, own(i)).start())
+        keep = pltpu.make_async_copy(x_ref, out_ref.at[pl.ds(half, half)], own_sem)
+        keep.start()
+        each(PIECES, lambda i: rightward(i, low(i)).wait_recv())
+        keep.wait()
+        each(PIECES, lambda i: leftward(i, own(i)).wait_send())
+
+    def pass_right(i):
+        moving = rightward(i, low(i))
+        moving.wait_recv()
+        moving.start()
+
+    def pass_left(i):
+        moving = leftward(i, high(i))
+        moving.wait_recv()
+        moving.start()
+
+    def finish(i):
+        rightward(i, low(i)).wait_send()
+        leftward(i, high(i)).wait_send()
+
+    relay(place, count, pass_right, pass_left, finish)
+
+
+def line_scatter_kernel(
+    count, x_ref, out_ref, got_right, got_left, sum_right, sum_left,
+    send_right, recv_right, send_left, recv_left,
+):
+    place = lax.axis_index("seq")
+    right, left = lax.rem(place + 1, count), lax.rem(place + count - 1, count)
+    half = out_ref.shape[0]
+    rows = half // PIECES
+    neighbour_barrier(place, count, right, left)
+
+    def cut(i):
+        return pl.ds(pl.multiple_of(i * rows, rows), rows)
+
+    def low(i):
+        return x_ref.at[cut(i)]
+
+    def high(i):
+        return x_ref.at[pl.ds(pl.multiple_of(half + i * rows, rows), rows)]
+
+    def rightward(i, source):
+        return send(source, got_right.at[cut(i)], send_right.at[i], recv_right.at[i], right)
+
+    def leftward(i, source):
+        return send(source, got_left.at[cut(i)], send_left.at[i], recv_left.at[i], left)
+
+    def added(got, mine):
+        return got[...].astype(jnp.float32) + mine[...].astype(jnp.float32)
+
+    @pl.when(place == 0)
+    def _():
+        each(PIECES, lambda i: rightward(i, high(i)).start())
+
+        def close(i):
+            leftward(i, low(i)).wait_recv()
+            out_ref[cut(i), :] = added(got_left.at[cut(i)], low(i))
+
+        each(PIECES, close)
+        each(PIECES, lambda i: rightward(i, high(i)).wait_send())
+
+    @pl.when(place == count - 1)
+    def _():
+        each(PIECES, lambda i: leftward(i, low(i)).start())
+
+        def close(i):
+            rightward(i, high(i)).wait_recv()
+            out_ref[cut(i), :] = added(got_right.at[cut(i)], high(i))
+
+        each(PIECES, close)
+        each(PIECES, lambda i: leftward(i, low(i)).wait_send())
+
+    def pass_right(i):
+        moving = rightward(i, sum_right.at[cut(i)])
+        moving.wait_recv()
+        sum_right[cut(i), :] = added(got_right.at[cut(i)], high(i)).astype(sum_right.dtype)
+        moving.start()
+
+    def pass_left(i):
+        moving = leftward(i, sum_left.at[cut(i)])
+        moving.wait_recv()
+        sum_left[cut(i), :] = added(got_left.at[cut(i)], low(i)).astype(sum_left.dtype)
+        moving.start()
+
+    def finish(i):
+        rightward(i, sum_right.at[cut(i)]).wait_send()
+        leftward(i, sum_left.at[cut(i)]).wait_send()
+        out_ref[cut(i), :] = jnp.zeros((rows, out_ref.shape[1]), out_ref.dtype)
+
+    relay(place, count, pass_right, pass_left, finish)
+
+
+def gather_rows(array):
+    half, width = array.shape
+    count = lax.axis_size("seq")
+    return pl.pallas_call(
+        functools.partial(line_gather_kernel, count),
+        in_specs=[pl.BlockSpec(memory_space=pltpu.VMEM)],
+        out_specs=pl.BlockSpec(memory_space=pltpu.VMEM),
+        out_shape=jax.ShapeDtypeStruct((2 * half, width), array.dtype),
+        scratch_shapes=[pltpu.SemaphoreType.DMA((PIECES,))] * 4 + [pltpu.SemaphoreType.DMA],
+        compiler_params=pltpu.CompilerParams(collective_id=0, has_side_effects=True),
+        cost_estimate=pl.CostEstimate(
+            flops=0, bytes_accessed=80 * half * width, transcendentals=0
+        ),
+        name="line_gather",
+    )(array)
+
+
+def scatter_rows(array):
+    rows, width = array.shape
+    half = rows // 2
+    count = lax.axis_size("seq")
+    return pl.pallas_call(
+        functools.partial(line_scatter_kernel, count),
+        in_specs=[pl.BlockSpec(memory_space=pltpu.VMEM)],
+        out_specs=pl.BlockSpec(memory_space=pltpu.VMEM),
+        out_shape=jax.ShapeDtypeStruct((half, width), jnp.float32),
+        scratch_shapes=[pltpu.VMEM((half, width), array.dtype)] * 4
+        + [pltpu.SemaphoreType.DMA((PIECES,))] * 4,
+        compiler_params=pltpu.CompilerParams(collective_id=1, has_side_effects=True),
+        cost_estimate=pl.CostEstimate(
+            flops=0, bytes_accessed=80 * half * width, transcendentals=0
+        ),
+        name="line_scatter",
+    )(array)
+
+
 def other_core(array):
     return lax.ppermute(array, "pipe", [(0, 1), (1, 0)])
 
@@ -260,58 +495,29 @@
     ).astype(kind)
 
 
-def gather_rows(array):
-    return lax.all_gather(array, "seq", axis=0, tiled=True)
-
-
-def scatter_rows(array):
-    return lax.psum_scatter(array, "seq", scatter_dimension=0, tiled=True).astype(jnp.float32)
-
-
-def pair_moves(step):
-    count = lax.axis_size("dp")
-    return [(i, i ^ step) for i in range(count)]
-
-
-def start_sum(grad):
+def core_half(grad):
     core = lax.axis_index("pipe")
-    row = lax.axis_index("dp")
-    count = lax.axis_size("dp")
     rows, columns = grad.shape
     halves = grad.reshape(2, rows // 2, columns)
     keep = lax.dynamic_index_in_dim(halves, core, 0, keepdims=False)
-    send = lax.dynamic_index_in_dim(halves, 1 - core, 0, keepdims=False)
-    half = (
-        keep.astype(jnp.float32) + other_core(send).astype(jnp.float32)
-    ).astype(jnp.bfloat16)
-    parts = half.reshape(count, rows // (2 * count), columns)
-    total = lax.dynamic_index_in_dim(parts, row, 0, keepdims=False).astype(jnp.float32)
-    for step in range(1, count):
-        away = lax.dynamic_index_in_dim(parts, row ^ step, 0, keepdims=False)
-        total = total + lax.ppermute(away, "dp", pair_moves(step)).astype(jnp.float32)
-    return total.astype(jnp.bfloat16)
+    away = lax.dynamic_index_in_dim(halves, 1 - core, 0, keepdims=False)
+    received = other_core(away)
+    return (keep.astype(jnp.float32) + received.astype(jnp.float32)).astype(jnp.bfloat16)
+
+
+def row_sum(halves, previous):
+    if previous is not None:
+        halves, previous = lax.optimization_barrier((halves, previous))
+    return lax.psum(halves, "dp"), previous
 
 
 def finish_sum(zero, one):
-    core = lax.axis_index("pipe")
-    row = lax.axis_index("dp")
-    count = lax.axis_size("dp")
-    first = core == 0
+    first = lax.axis_index("pipe") == 0
     own = pick(first, zero, one)
-    swapped = other_core(pick(first, one, zero))
-    rows, columns = own.shape
-    whole = jnp.zeros((2, count, rows, columns), jnp.float32)
-
-    def put(whole, piece, half, place):
-        return lax.dynamic_update_slice(
-            whole, piece.astype(jnp.float32)[None, None], (half, place, 0, 0)
-        )
-
-    for half, piece in ((core, own), (1 - core, swapped)):
-        whole = put(whole, piece, half, row)
-        for step in range(1, count):
-            whole = put(whole, lax.ppermute(piece, "dp", pair_moves(step)), half, row ^ step)
-    return whole.reshape(2 * count * rows, columns)
+    received = other_core(pick(first, one, zero))
+    return jnp.concatenate([pick(first, own, received), pick(first, received, own)]).astype(
+        jnp.float32
+    )
 
 
 def body(
@@ -333,41 +539,67 @@
     local_rows, width = inputs.shape[2], inputs.shape[3]
     local_width = w_query.shape[2]
     hidden_here = w_gate.shape[2]
+    line = lax.axis_size("seq")
+    slots = local_rows * line
+    half = slots // 2
     core = lax.axis_index("pipe")
     row = lax.axis_index("dp")
     place = lax.axis_index("seq")
     first = core == 0
     bf16 = jnp.bfloat16
+    at_end = jnp.logical_or(place == 0, place == line - 1)
+    at_end_weight = at_end.astype(jnp.float32)
+    half_start = (place >= line // 2).astype(jnp.int32) * half
+
+    def own_half(array):
+        return lax.dynamic_slice_in_dim(array, half_start, half, 0)
+
+    def own_rows(array):
+        return lax.dynamic_slice_in_dim(array, place * local_rows, local_rows, 0)
+
+    def from_ends(array):
+        if line > 4:
+            whole = lax.all_gather(array, "seq", axis=0, tiled=False)
+            return own_rows(jnp.concatenate([whole[0], whole[line - 1]]))
+        quarters = array.reshape(2, local_rows, width)
+        moved = lax.ppermute(
+            pick(place == 0, quarters[1], quarters[0]), "seq", [(0, 1), (3, 2)]
+        )
+        kept = pick(place == 0, quarters[0], quarters[1])
+        return pick(at_end, kept, moved)
+
+    def gather_all(array):
+        return lax.all_gather(array, "seq", axis=0, tiled=True)
 
     def both(array):
         return lax.all_gather(array, "pipe", axis=0, tiled=False)
 
+    block_in = gather_all(lax.dynamic_index_in_dim(inputs, core, 0, keepdims=False)[0])
+    gains = both(jnp.stack([norm_gain[0], ffn_gain[0]]))
+    bounds = both(jnp.stack([lower_bound[0], out_gain[0]]))
     w_proj_both = both(jnp.concatenate([w_query[0], w_forget[0], w_input[0]], axis=1).astype(bf16))
     w_out_both = both(w_output[0].astype(bf16))
     w_pair_both = both(jnp.concatenate([w_gate[0], w_up[0]], axis=1).astype(bf16))
     w_down_both = both(w_down[0].astype(bf16))
-    gains = both(jnp.stack([norm_gain[0], ffn_gain[0]]))
-    bounds = both(jnp.stack([lower_bound[0], out_gain[0]]))
 
     own_length = lax.dynamic_slice(lengths, (core, row), (1, 1))[0, 0]
-    positions = place * local_rows + jnp.arange(local_rows, dtype=jnp.int32)
-    mask = (positions < own_length).astype(jnp.float32)[:, None]
-    block_in = lax.dynamic_index_in_dim(inputs, core, 0, keepdims=False)[0]
-    source_grad = lax.dynamic_index_in_dim(cotangent, core, 0, keepdims=False)[0]
+    mask_all = (jnp.arange(slots, dtype=jnp.int32) < own_length).astype(jnp.float32)[:, None]
+    mask = own_half(mask_all)
+    source_grad = gather_all(lax.dynamic_index_in_dim(cotangent, core, 0, keepdims=False)[0])
 
     saved = []
     outs = []
     for section in range(2):
-        residual = block_in.astype(jnp.float32)
-        normed = (residual * inverse_rms(residual) * gains[section, 0]).astype(bf16)
-        normed_all = gather_rows(normed)
+        residual_all = block_in.astype(jnp.float32)
+        normed_all = (residual_all * inverse_rms(residual_all) * gains[section, 0]).astype(bf16)
+        residual_low = own_half(block_in)
+        residual = residual_low.astype(jnp.float32)
         projected = dot(normed_all, w_proj_both[section], 1, 0)
         head_gain = bounds[section, 1]
         mixed_gain, squares, states = rec_fwd(projected, bounds[section, 0], head_gain)
         squares = small_sum(squares[0], "seq")
         branch = scatter_rows(dot(mixed_gain, w_out_both[section], 1, 0, bf16))
-        own_squares = lax.dynamic_slice(squares, (place * local_rows,), (local_rows,))
-        inv_mix = lax.rsqrt(own_squares / width + EPSILON)[:, None]
+        inv_mix = lax.rsqrt(own_half(squares) / width + EPSILON)[:, None]
         branch = branch * inv_mix
         middle = residual + branch
         normed_two = (middle * inverse_rms(middle) * gains[section, 1]).astype(bf16)
@@ -378,25 +610,29 @@
         hidden = (jax.nn.silu(gate_act) * up_act).astype(bf16)
         ffn_branch = scatter_rows(dot(hidden, w_down_both[section], 1, 0, bf16))
         out_low = (mask * (middle + ffn_branch)).astype(bf16)
-        outs.append(out_low)
         saved.append(
-            (residual, normed_all, projected, mixed_gain, states, inv_mix, branch, middle)
+            (residual_low, normed_all, projected, mixed_gain, states, inv_mix, branch, middle)
             + (normed_two_all, paired, hidden)
         )
-        block_in = out_low
+        if section == 0:
+            block_in = gather_rows(out_low)
+            outs.append(own_rows(block_in))
+        else:
+            outs.append(from_ends(out_low))
 
     small = [None, None]
-    shares = [None, None]
+    sums = [None, None]
     grad_ins = [None, None]
-    grad_out = source_grad.astype(jnp.float32)
+    summed = None
+    grad_branch_all = (mask_all * source_grad.astype(jnp.float32)).astype(bf16)
+    masked = own_half(grad_branch_all).astype(jnp.float32)
     for section in (1, 0):
-        residual, normed_all, projected, mixed_gain, states, inv_mix, branch, middle = saved[
+        residual_low, normed_all, projected, mixed_gain, states, inv_mix, branch, middle = saved[
             section
         ][:8]
+        residual = residual_low.astype(jnp.float32)
         normed_two_all, paired, hidden = saved[section][8:]
         head_gain = bounds[section, 1]
-        masked = mask * grad_out
-        grad_branch_all = gather_rows(masked.astype(bf16))
         grad_hidden = dot(grad_branch_all, w_down_both[section], 1, 1)
         gate_act = paired[:, :hidden_here].astype(jnp.float32)
         up_act = paired[:, hidden_here:].astype(jnp.float32)
@@ -404,19 +640,18 @@
         grad_up = grad_hidden * gate_act * sig
         grad_gate = grad_hidden * up_act * sig * (1.0 + gate_act * (1.0 - sig))
         grad_pair = jnp.concatenate([grad_gate.astype(bf16), grad_up.astype(bf16)], axis=1)
+        grad_down = core_half(dot(hidden, grad_branch_all, 0, 0, bf16))
+        grad_pair_weight = core_half(dot(normed_two_all, grad_pair, 0, 0, bf16))
+        ffn_sums, previous = row_sum((grad_down, grad_pair_weight), summed)
+        if previous is not None:
+            sums[1] = sums[1][:1] + [previous]
         grad_normed_two = scatter_rows(dot(grad_pair, w_pair_both[section], 1, 1, bf16))
-        grad_down = dot(hidden, grad_branch_all, 0, 0, bf16)
-        grad_pair_weight = dot(normed_two_all, grad_pair, 0, 0, bf16)
         from_norm, grad_gain_two = norm_backward(middle, gains[section, 1], grad_normed_two)
         grad_middle = masked + from_norm
         inner = jnp.sum(grad_middle * branch, axis=1)
-        factor = inv_mix[:, 0] * inv_mix[:, 0] * inner / width
+        factor = inv_mix[:, 0] * inv_mix[:, 0] * inner * (at_end_weight / width)
         factor_all = small_sum(
-            lax.dynamic_update_slice(
-                jnp.zeros((local_rows * lax.axis_size("seq"),), jnp.float32),
-                factor,
-                (place * local_rows,),
-            ),
+            lax.dynamic_update_slice(jnp.zeros((slots,), jnp.float32), factor, (half_start,)),
             "seq",
         )
         grad_mix_all = gather_rows((grad_middle * inv_mix).astype(bf16))
@@ -425,28 +660,33 @@
         grad_head_gain = jnp.sum(grad_head * mixed, axis=0)
         grad_mixed = (grad_head * head_gain - mixed * factor_all[:, None]).astype(bf16)
         grad_proj, grad_bound = rec_bwd(projected, states, grad_mixed, bounds[section, 0])
+        grad_out_weight = core_half(dot(mixed_gain, grad_mix_all, 0, 0, bf16))
+        grad_proj_weight = core_half(dot(normed_all, grad_proj, 0, 0, bf16))
+        mix_sums, ffn_sums = row_sum((grad_out_weight, grad_proj_weight), ffn_sums)
+        summed = mix_sums
+        sums[section] = [ffn_sums, mix_sums]
         grad_normed = scatter_rows(dot(grad_proj, w_proj_both[section], 1, 1, bf16))
-        grad_out_weight = dot(mixed_gain, grad_mix_all, 0, 0, bf16)
-        grad_proj_weight = dot(normed_all, grad_proj, 0, 0, bf16)
         from_first, grad_gain_one = norm_backward(residual, gains[section, 0], grad_normed)
         grad_in = grad_middle + from_first
-        grad_ins[section] = grad_in
-        grad_out = grad_in.astype(bf16).astype(jnp.float32)
+        grad_ins[section] = from_ends(grad_in)
+        if section == 1:
+            masked_low = (mask * grad_in).astype(bf16)
+            masked = masked_low.astype(jnp.float32)
+            grad_branch_all = gather_rows(masked_low)
         spread = jnp.zeros((2, width), jnp.float32)
         spread = lax.dynamic_update_slice(
             spread, jnp.stack([grad_bound, grad_head_gain]), (0, place * local_width)
         )
-        small[section] = jnp.concatenate([jnp.stack([grad_gain_one, grad_gain_two]), spread])
-        shares[section] = [
-            start_sum(part)
-            for part in (grad_down, grad_pair_weight, grad_out_weight, grad_proj_weight)
-        ]
-
-    small_total = lax.psum(jnp.stack(small), ("pipe", "seq", "dp"))
-    small_own = lax.dynamic_index_in_dim(small_total, core, 0, keepdims=False)
+        partial = jnp.concatenate(
+            [jnp.stack([grad_gain_one, grad_gain_two]) * at_end_weight, spread]
+        )
+        small[section] = small_sum(small_sum(small_sum(partial, "pipe"), "seq"), "dp")
+
+    small_own = pick(first, small[0], small[1])
     local_small = lax.dynamic_slice(small_own, (2, place * local_width), (2, local_width))
+    zeros, ones = [group[0] + group[1] for group in sums]
     grad_down, grad_pair_weight, grad_out_weight, grad_proj_weight = [
-        finish_sum(zero, one) for zero, one in zip(shares[0], shares[1])
+        finish_sum(zero, one) for zero, one in zip(zeros, ones)
     ]
 
     def exchange(zero, one):

time: 2140 us -> 1950 us (0.911)
  waiting for transfers between devices: 1400 us -> 388 us
  Pallas kernels: 67.6 us -> 921 us
  starting transfers between devices: 74.4 us -> 38.9 us
  other arithmetic: 186 us -> 219 us
  local copies, waits for them, and re-layouts: 109 us -> 84 us
    pallas_call x0 -> x14, Pallas kernels: none -> 854 us  [the longest x8 481 us: scatter_rows(): pl.pallas_call(functools.partial(line_scatter_kernel, count), in_specs=[p...]
    all_gather x8 -> x2, waiting for transfers between devices: 486 us -> 112 us  [gather_all(): return lax.all_gather(array, 'seq', axis=0, tiled=True)]
    reduce_scatter x8 -> x0, waiting for transfers between devices: 330 us -> none  [scatter_rows(): lax.psum_scatter(array, 'seq', scatter_dimension=0, tiled=True)]
    ppermute x48 -> x3, waiting for transfers between devices: 395 us -> 92.2 us  [from_ends(): lax.ppermute(pick(place == 0, quarters[1], quarters[0]), 'seq', [(0, 1),...]
    psum x1 -> x4, waiting for transfers between devices: 107 us -> 158 us  [row_sum(): return (lax.psum(halves, 'dp'), previous)]
    ppermute x48 -> x3, starting transfers between devices: 56.5 us -> 6.43 us  [from_ends(): lax.ppermute(pick(place == 0, quarters[1], quarters[0]), 'seq', [(0, 1),...]
    dynamic_update_slice x34 -> x2, other arithmetic: 46.2 us -> 0.38 us  [body(): lax.dynamic_update_slice(jnp.zeros((slots,), jnp.float32), factor, (half_...]
    convert_element_type x12 -> x16, other arithmetic: 35.9 us -> 81.7 us  [the longest x8 41.1 us: core_half(): (keep.astype(jnp.float32) + received.astype(jnp.float32)).astype(jnp.bflo...]
  transfers between devices with their start and end apart: 95 -> 53, of which waited for: 52 -> 13; matrix products, arithmetic and copies ran while one was open for 21% -> 21% of each run, Pallas kernels for 2% -> 32%
where the time goes in v2:
time: 1950 us; the launch traced here: 1940 us
  Pallas kernels  921 us (47%)
  waiting for transfers between devices  388 us (20%)
  matrix products  271 us (14%)
  other arithmetic  219 us (11%)
  local copies, waits for them, and re-layouts  84 us (4%)
  starting transfers between devices  38.9 us (2%)
    pallas_call x8, Pallas kernels, scatter_rows(): pl.pallas_call(functools.partial(line_scatter_kernel, count), in_specs=[p...  481 us
    pallas_call x6, Pallas kernels, gather_rows(): pl.pallas_call(functools.partial(line_gather_kernel, count), in_specs=[pl...  373 us
    dot_general x24, matrix products, dot(): lax.dot_general(left, right, (((left_dim,), (right_dim,)), ((), ())), pre...  271 us
    psum x4, waiting for transfers between devices, row_sum(): return (lax.psum(halves, 'dp'), previous)  158 us
    all_gather x2, waiting for transfers between devices, gather_all(): return lax.all_gather(array, 'seq', axis=0, tiled=True)  112 us
    ppermute x3, waiting for transfers between devices, from_ends(): lax.ppermute(pick(place == 0, quarters[1], quarters[0]), 'seq', [(0, 1),...  92.2 us
    convert_element_type x8, other arithmetic, core_half(): (keep.astype(jnp.float32) + received.astype(jnp.float32)).astype(jnp.bflo...  41.1 us
  transfers between devices with their start and end apart: 53, of which 13 were waited for; matrix products, arithmetic and copies ran while one was open for 21% of the time, Pallas kernels for 32%

profile of v2, /device:TPU:0, one launch (start us, length us, event | category | flops | bytes accessed | tf_op | source)
XLA Modules:
  0.0 1940.9 jit_solution(4897360614425188375)
XLA Ops:
  30.4 7.4 convert.27
  37.8 7.9 pad_maximum_fusion
  45.8 7.7 convert_element_type.321
  60.1 33.6 %all-gather.21.cloned.1.call-done = bf16[1,1,1024,2048]{3,2,1,0:T(8,128)(2,1)} async-done(((bf16[1,1,256,2048]{3,2,1,0:T(8,128)(2,1)}), bf16[1,1,1024,2048]{3,2,1,0:T(8,128)(2,1)}) %all-gather.21.cloned.1.call-update) | async-done | bytes 4194320 | tf_op jit(solution)/shard_map/all_gather | solution.py:572
  96.7 78.3 %all-gather.23.cloned.1.call-done = bf16[1,1,1024,2048]{3,2,1,0:T(8,128)(2,1)} async-done(((bf16[1,1,256,2048]{3,2,1,0:T(8,128)(2,1)}), bf16[1,1,1024,2048]{3,2,1,0:T(8,128)(2,1)}) %all-gather.23.cloned.1.call-update) | async-done | bytes 4194320 | tf_op jit(solution)/shard_map/all_gather | solution.py:572
  180.0 20.4 %all-gather.13.cloned.1.call-done = bf16[2,2048,1536]{2,1,0:T(8,128)(2,1)} async-done(((bf16[1,2048,1536]{2,1,0:T(8,128)(2,1)}), bf16[2,2048,1536]{2,1,0:T(8,128)(2,1)}) %all-gather.13.cloned.1.call-update) | async-done | bytes 12582928 | tf_op jit(solution)/shard_map/all_gather | solution.py:575
  200.4 11.8 fusion.46.proj_ref
  212.2 15.4 rec_fwd.2
  233.0 7.6 convolution_convert_fusion.7.x_ref
  240.5 65.0 %line_scatter.8 = f32[512,2048]{1,0:T(8,128)} custom-call(bf16[1024,2048]{1,0:T(8,128)(2,1)} %convolution_convert_fusion.7.x_ref), custom_call_target="tpu_custom_call" | custom-call | bytes 83886080 | tf_op jit(solution)/shard_map/line_scatter/pallas_call | solution.py:447
  313.5 59.8 %line_gather.6 = bf16[1024,2048]{1,0:T(8,128)(2,1)} custom-call(bf16[512,2048]{1,0:T(8,128)(2,1)} %multiply_convert_fusion.6.x_ref), custom_call_target="tpu_custom_call" | custom-call | bytes 83886080 | tf_op jit(solution)/shard_map/line_gather/pallas_call | solution.py:429
  373.8 18.5 fusion.44
  392.4 12.4 fusion.68.x_ref
  404.8 59.4 %line_scatter.9 = f32[512,2048]{1,0:T(8,128)} custom-call(bf16[1024,2048]{1,0:T(8,128)(2,1)} %fusion.68.x_ref), custom_call_target="tpu_custom_call" | custom-call | bytes 83886080 | tf_op jit(solution)/shard_map/line_scatter/pallas_call | solution.py:447
  469.4 68.9 %line_gather.7 = bf16[1024,2048]{1,0:T(8,128)(2,1)} custom-call(bf16[512,2048]{1,0:T(8,128)(2,1)} %multiply_convert_fusion.5.x_ref), custom_call_target="tpu_custom_call" | custom-call | bytes 83886080 | tf_op jit(solution)/shard_map/line_gather/pallas_call | solution.py:429
  541.7 10.6 fusion.48.proj_ref
  552.3 15.2 rec_fwd.3
  570.5 6.3 convolution_convert_fusion.6.x_ref
  576.7 59.3 %line_scatter.10 = f32[512,2048]{1,0:T(8,128)} custom-call(bf16[1024,2048]{1,0:T(8,128)(2,1)} %convolution_convert_fusion.6.x_ref), custom_call_target="tpu_custom_call" | custom-call | bytes 83886080 | tf_op jit(solution)/shard_map/line_scatter/pallas_call | solution.py:447
  643.9 55.5 %line_gather.8 = bf16[1024,2048]{1,0:T(8,128)(2,1)} custom-call(bf16[512,2048]{1,0:T(8,128)(2,1)} %multiply_convert_fusion.4.x_ref), custom_call_target="tpu_custom_call" | custom-call | bytes 83886080 | tf_op jit(solution)/shard_map/line_gather/pallas_call | solution.py:429
  699.4 17.0 fusion.43
  718.9 11.3 fusion.67.x_ref
  730.2 55.4 %line_scatter.11 = f32[512,2048]{1,0:T(8,128)} custom-call(bf16[1024,2048]{1,0:T(8,128)(2,1)} %fusion.67.x_ref), custom_call_target="tpu_custom_call" | custom-call | bytes 83886080 | tf_op jit(solution)/shard_map/line_scatter/pallas_call | solution.py:447
  785.6 12.5 convolution_convert_fusion.2
  798.1 12.2 fusion.28
  812.9 16.2 fusion.65.x_ref
  829.1 54.5 %line_scatter.12 = f32[512,2048]{1,0:T(8,128)} custom-call(bf16[1024,2048]{1,0:T(8,128)(2,1)} %fusion.65.x_ref), custom_call_target="tpu_custom_call" | custom-call | bytes 83886080 | tf_op jit(solution)/shard_map/line_scatter/pallas_call | solution.py:447
  897.2 19.8 %convolution_convert_fusion = bf16[2048,2816]{1,0:T(8,128)(2,1)} fusion(bf16[1024,2048]{1,0:T(8,128)(2,1)} %line_gather.8, bf16[1024,1408]{1,0:T(8,128)(2,1)} %copy-done.76, bf16[1024,1408]{1,0:T(8,128)(2,1)} %copy-done.75), kind=kOutput, calls=%fused_computation.10 | convolution fusion | flops 11828461568 | bytes 21495808 | tf_op jit(solution)/shard_map/dot_general | solution.py:493
  921.5 62.6 %line_gather.9 = bf16[1024,2048]{1,0:T(8,128)(2,1)} custom-call(bf16[512,2048]{1,0:T(8,128)(2,1)} %multiply_convert_fusion.2.x_ref), custom_call_target="tpu_custom_call" | custom-call | bytes 83886080 | tf_op jit(solution)/shard_map/line_gather/pallas_call | solution.py:429
  990.0 6.1 dynamic-slice_bitcast_fusion
  1000.8 18.3 rec_bwd.2
  1019.1 11.1 fusion.69.x_ref
  1030.1 62.7 %line_scatter.13 = f32[512,2048]{1,0:T(8,128)} custom-call(bf16[1024,2048]{1,0:T(8,128)(2,1)} %fusion.69.x_ref), custom_call_target="tpu_custom_call" | custom-call | bytes 83886080 | tf_op jit(solution)/shard_map/line_scatter/pallas_call | solution.py:447
  1097.0 6.1 multiply_convert_fusion.1
  1103.0 61.2 %line_gather.10 = bf16[1024,2048]{1,0:T(8,128)(2,1)} custom-call(bf16[512,2048]{1,0:T(8,128)(2,1)} %get-tuple-element.104.x_ref), custom_call_target="tpu_custom_call" | custom-call | bytes 83886080 | tf_op jit(solution)/shard_map/line_gather/pallas_call | solution.py:429
  1164.3 13.3 fusion.24
  1180.0 16.3 fusion.66.x_ref
  1196.2 60.7 %line_scatter.14 = f32[512,2048]{1,0:T(8,128)} custom-call(bf16[1024,2048]{1,0:T(8,128)(2,1)} %fusion.66.x_ref), custom_call_target="tpu_custom_call" | custom-call | bytes 83886080 | tf_op jit(solution)/shard_map/line_scatter/pallas_call | solution.py:447
  1270.6 17.3 convolution_convert_fusion.1
  1293.2 8.2 fusion
  1302.0 9.9 convolution_convert_fusion.3
  1318.7 65.0 %line_gather.11 = bf16[1024,2048]{1,0:T(8,128)(2,1)} custom-call(bf16[512,2048]{1,0:T(8,128)(2,1)} %multiply_convert_fusion.x_ref), custom_call_target="tpu_custom_call" | custom-call | bytes 83886080 | tf_op jit(solution)/shard_map/line_gather/pallas_call | solution.py:429
  1383.8 5.7 dynamic-slice_bitcast_fusion.1
  1392.4 10.4 convolution_convert_fusion.4
  1417.0 18.5 rec_bwd.3
  1444.4 32.3 %all-reduce.15.cloned.1.call-done = (bf16[704,2048]{1,0:T(8,128)(2,1)}, bf16[1024,2816]{1,0:T(8,128)(2,1)}) async-done(((bf16[704,2048]{1,0:T(8,128)(2,1)}, bf16[1024,2816]{1,0:T(8,128)(2,1)}), (bf16[704,2048]{1,0:T(8,128)(2,1)}, bf16[1024,2816]{1,0:T(8,128)(2,1)})) %all-reduce.15.cloned.1.call-update) | async-done | bytes 8650768 | tf_op jit(solution)/shard_map/psum | solution.py:511
  1476.8 11.1 fusion.70.x_ref
  1487.9 63.7 %line_scatter.15 = f32[512,2048]{1,0:T(8,128)} custom-call(bf16[1024,2048]{1,0:T(8,128)(2,1)} %fusion.70.x_ref), custom_call_target="tpu_custom_call" | custom-call | bytes 83886080 | tf_op jit(solution)/shard_map/line_scatter/pallas_call | solution.py:447
  1555.8 5.7 fusion.42
  1561.6 8.3 fusion.1
  1569.9 14.6 all-reduce.13.cloned.1.call-done
  1585.2 10.0 convolution_convert_fusion.5
  1630.9 12.1 collective-permute-done.6
  1647.4 40.5 %collective-permute-done.15 = f32[256,2048]{1,0:T(8,128)S(1)} collective-permute-done((f32[256,2048]{1,0:T(8,128)S(1)}, f32[256,2048]{1,0:T(8,128)S(1)}, u32[]{:S(2)}, u32[]{:S(2)}) %collective-permute-start.15) | collective-permute-done | bytes 2097184 | tf_op jit(solution)/shard_map/ppermute | solution.py:565
  1689.3 39.6 %collective-permute-done.14 = f32[256,2048]{1,0:T(8,128)} collective-permute-done((f32[256,2048]{1,0:T(8,128)S(1)}, f32[256,2048]{1,0:T(8,128)}, u32[]{:S(2)}, u32[]{:S(2)}) %collective-permute-start.14) | collective-permute-done | bytes 2097184 | tf_op jit(solution)/shard_map/ppermute | solution.py:565
  1737.5 29.7 %all-reduce.11.cloned.1.call-done = (bf16[704,2048]{1,0:T(8,128)(2,1)}, bf16[1024,2816]{1,0:T(8,128)(2,1)}) async-done(((bf16[704,2048]{1,0:T(8,128)(2,1)}, bf16[1024,2816]{1,0:T(8,128)(2,1)}), (bf16[704,2048]{1,0:T(8,128)(2,1)}, bf16[1024,2816]{1,0:T(8,128)(2,1)})) %all-reduce.11.cloned.1.call-update) | async-done | bytes 8650768 | tf_op jit(solution)/shard_map/psum | solution.py:511
  1771.4 5.8 broadcast_select_fusion.2
  1793.9 80.9 %all-reduce.9.cloned.1.call-done = (bf16[1024,1536]{1,0:T(8,128)(2,1)}, bf16[256,2048]{1,0:T(8,128)(2,1)}) async-done(((bf16[1024,1536]{1,0:T(8,128)(2,1)}, bf16[256,2048]{1,0:T(8,128)(2,1)}), (bf16[1024,1536]{1,0:T(8,128)(2,1)}, bf16[256,2048]{1,0:T(8,128)(2,1)})) %all-reduce.9.cloned.1.call-update) | async-done | bytes 4194320 | tf_op jit(solution)/shard_map/psum | solution.py:511
  1876.6 7.9 maximum_convert_fusion.2
  1891.5 7.4 broadcast_select_fusion.1
  1898.9 6.9 maximum_convert_fusion
  1905.8 8.4 slice_bitcast_fusion
  1917.6 6.4 maximum_convert_fusion.1
  1923.9 9.9 slice_bitcast_fusion.24
  (392 shorter events, 251.0 us)
Async XLA Ops:
  7.2 86.4 %all-gather.21.cloned.1.call-start = ((), (), s32[]{:S(2)}) async-start(), calls=%async_computation.4 | async-start | bytes 5242880 | tf_op jit(solution)/shard_map/all_gather | solution.py:572
  9.9 165.2 %all-gather.23.cloned.1.call-start = ((), (), s32[]{:S(2)}) async-start(), calls=%async_computation.5 | async-start | bytes 5242880 | tf_op jit(solution)/shard_map/all_gather | solution.py:572
  12.3 188.1 %all-gather.13.cloned.1.call-start = ((), (), s32[]{:S(2)}) async-start(), calls=%async_computation | async-start | bytes 18874368 | tf_op jit(solution)/shard_map/all_gather | solution.py:575
  21.2 211.7 %all-gather.15.cloned.1.call-start = ((), (), s32[]{:S(2)}) async-start(), calls=%async_computation.1 | async-start | bytes 6291456 | tf_op jit(solution)/shard_map/all_gather | solution.py:575
  25.4 348.4 %all-gather.17.cloned.1.call-start = ((), (), s32[]{:S(2)}) async-start(), calls=%async_computation.2 | async-start | bytes 34603008 | tf_op jit(solution)/shard_map/all_gather | solution.py:575
  45.7 346.7 %all-gather.19.cloned.1.call-start = ((), (), s32[]{:S(2)}) async-start(), calls=%async_computation.3 | async-start | bytes 17301504 | tf_op jit(solution)/shard_map/all_gather | solution.py:575
  53.5 1423.3 %all-reduce.15.cloned.1.call-start = ((), (), s32[]{:S(2)}) async-start(), calls=%async_computation.9 | async-start | bytes 17301504 | tf_op jit(solution)/shard_map/psum | solution.py:511
  60.0 140.4 %copy-start.48 = (f32[1,1,2048]{2,1,0:T(1,128)}, f32[1,1,2048]{2,1,0:T(1,128)S(1)}, u32[]{:S(2)}) copy-start(f32[1,1,2048]{2,1,0:T(1,128)S(1)} %get-tuple-element.149) | copy-start | bytes 24580
  60.0 249.7 %copy-start.46 = (f32[1,1,2048]{2,1,0:T(1,128)}, f32[1,1,2048]{2,1,0:T(1,128)S(1)}, u32[]{:S(2)}) copy-start(f32[1,1,2048]{2,1,0:T(1,128)S(1)} %get-tuple-element.148) | copy-start | bytes 24580
  60.0 481.4 %copy-start.50 = (f32[1,1,2048]{2,1,0:T(1,128)}, f32[1,1,2048]{2,1,0:T(1,128)S(1)}, u32[]{:S(2)}) copy-start(f32[1,1,2048]{2,1,0:T(1,128)S(1)} %get-tuple-element.147) | copy-start | bytes 24580
  96.7 103.7 %copy-start.62 = (f32[1024]{0:T(1024)}, f32[1024]{0:T(1024)S(1)}, u32[]{:S(2)}) copy-start(f32[1024]{0:T(1024)S(1)} %add_rsqrt_fusion.1) | copy-start | bytes 12292
  228.3 77.3 %collective-permute-start.2 = (f32[1024]{0:T(1024)S(1)}, f32[1024]{0:T(1024)S(1)}, u32[]{:S(2)}, u32[]{:S(2)}) collective-permute-start(f32[1024]{0:T(1024)S(1)} %bitcast.244), channel_id=1, source_target_pairs={{0,12},{4,0},{8,4},{12,8},{1,13},{5,1},{9,5},{13,9},{2,14},{6,2},{... | collective-permute-start | bytes 12296 | tf_op jit(solution)/shard_map/ppermute | solution.py:472
  231.9 73.7 %collective-permute-start.1 = (f32[1024]{0:T(1024)S(1)}, f32[1024]{0:T(1024)S(1)}, u32[]{:S(2)}, u32[]{:S(2)}) collective-permute-start(f32[1024]{0:T(1024)S(1)} %bitcast.245), channel_id=1, source_target_pairs={{0,8},{4,12},{8,0},{12,4},{1,9},{5,13},{9,1},{13,5},{2,10},{6,14},... | collective-permute-start | bytes 12296 | tf_op jit(solution)/shard_map/ppermute | solution.py:472
  231.9 73.7 %collective-permute-start = (f32[1024]{0:T(1024)S(1)}, f32[1024]{0:T(1024)S(1)}, u32[]{:S(2)}, u32[]{:S(2)}) collective-permute-start(f32[1024]{0:T(1024)S(1)} %bitcast.246), channel_id=1, source_target_pairs={{0,4},{4,8},{8,12},{12,0},{1,5},{5,9},{9,13},{13,1},{2,6},{6,10},{... | collective-permute-start | bytes 12296 | tf_op jit(solution)/shard_map/ppermute | solution.py:472
  309.7 63.5 %copy-start.55 = (f32[512]{0:T(512)}, f32[512]{0:T(512)S(1)}, u32[]{:S(2)}) copy-start(f32[512]{0:T(512)S(1)} %add_rsqrt_fusion.6) | copy-start | bytes 6148
  568.3 67.7 %collective-permute-start.5 = (f32[1024]{0:T(1024)S(1)}, f32[1024]{0:T(1024)S(1)}, u32[]{:S(2)}, u32[]{:S(2)}) collective-permute-start(f32[1024]{0:T(1024)S(1)} %bitcast.248), channel_id=1, source_target_pairs={{0,12},{4,0},{8,4},{12,8},{1,13},{5,1},{9,5},{13,9},{2,14},{6,2},{... | collective-permute-start | bytes 12296 | tf_op jit(solution)/shard_map/ppermute | solution.py:472
  569.9 66.2 %collective-permute-start.4 = (f32[1024]{0:T(1024)S(1)}, f32[1024]{0:T(1024)S(1)}, u32[]{:S(2)}, u32[]{:S(2)}) collective-permute-start(f32[1024]{0:T(1024)S(1)} %bitcast.249), channel_id=1, source_target_pairs={{0,8},{4,12},{8,0},{12,4},{1,9},{5,13},{9,1},{13,5},{2,10},{6,14},... | collective-permute-start | bytes 12296 | tf_op jit(solution)/shard_map/ppermute | solution.py:472
  569.9 66.2 %collective-permute-start.3 = (f32[1024]{0:T(1024)S(1)}, f32[1024]{0:T(1024)S(1)}, u32[]{:S(2)}, u32[]{:S(2)}) collective-permute-start(f32[1024]{0:T(1024)S(1)} %bitcast.250), channel_id=1, source_target_pairs={{0,4},{4,8},{8,12},{12,0},{1,5},{5,9},{9,13},{13,1},{2,6},{6,10},{... | collective-permute-start | bytes 12296 | tf_op jit(solution)/shard_map/ppermute | solution.py:472
  895.1 101.7 %collective-permute-start.10 = (f32[1024]{0:T(1024)S(1)}, f32[1024]{0:T(1024)S(1)}, u32[]{:S(2)}, u32[]{:S(2)}) collective-permute-start(f32[1024]{0:T(1024)S(1)} %fusion.80), channel_id=1, source_target_pairs={{0,12},{4,0},{8,4},{12,8},{1,13},{5,1},{9,5},{13,9},{2,14},{6,2},{... | collective-permute-start | bytes 12296 | tf_op jit(solution)/shard_map/ppermute | solution.py:472
  896.0 100.8 %collective-permute-start.9 = (f32[1024]{0:T(1024)S(1)}, f32[1024]{0:T(1024)S(1)}, u32[]{:S(2)}, u32[]{:S(2)}) collective-permute-start(f32[1024]{0:T(1024)S(1)} %fusion.80), channel_id=1, source_target_pairs={{0,8},{4,12},{8,0},{12,4},{1,9},{5,13},{9,1},{13,5},{2,10},{6,14},... | collective-permute-start | bytes 12296 | tf_op jit(solution)/shard_map/ppermute | solution.py:472
  896.0 100.0 %collective-permute-start.8 = (f32[1024]{0:T(1024)S(1)}, f32[1024]{0:T(1024)S(1)}, u32[]{:S(2)}, u32[]{:S(2)}) collective-permute-start(f32[1024]{0:T(1024)S(1)} %fusion.80), channel_id=1, source_target_pairs={{0,4},{4,8},{8,12},{12,0},{1,5},{5,9},{9,13},{13,1},{2,6},{6,10},{... | collective-permute-start | bytes 12296 | tf_op jit(solution)/shard_map/ppermute | solution.py:472
  918.8 369.2 %collective-permute-start.37 = (bf16[704,2048]{1,0:T(8,128)(2,1)}, bf16[704,2048]{1,0:T(8,128)(2,1)}, u32[]{:S(2)}, u32[]{:S(2)}) collective-permute-start(bf16[704,2048]{1,0:T(8,128)(2,1)} %dynamic-slice_bitcast_fusion.4), channel_id=1, source_target_pairs={{0,16},{16,0},{1,17},{17,1},{2,18},{18,2},{3,19},{19,3},{4,20},{20... | collective-permute-start | bytes 8650760 | tf_op jit(solution)/shard_map/ppermute | solution.py:463
  990.0 446.3 %collective-permute-start.35 = (bf16[256,2048]{1,0:T(8,128)(2,1)}, bf16[256,2048]{1,0:T(8,128)(2,1)}, u32[]{:S(2)}, u32[]{:S(2)}) collective-permute-start(bf16[256,2048]{1,0:T(8,128)(2,1)} %dynamic-slice_bitcast_fusion.6), channel_id=1, source_target_pairs={{0,16},{16,0},{1,17},{17,1},{2,18},{18,2},{3,19},{19,3},{4,20},{20... | collective-permute-start | bytes 3145736 | tf_op jit(solution)/shard_map/ppermute | solution.py:463
  996.1 297.1 %collective-permute-start.38 = (bf16[1024,2816]{1,0:T(8,128)(2,1)}, bf16[1024,2816]{1,0:T(8,128)(2,1)}, u32[]{:S(2)}, u32[]{:S(2)}) collective-permute-start(bf16[1024,2816]{1,0:T(8,128)(2,1)} %dynamic-slice_bitcast_fusion), channel_id=1, source_target_pairs={{0,16},{16,0},{1,17},{17,1},{2,18},{18,2},{3,19},{19,3},{4,20},{20... | collective-permute-start | bytes 17301512 | tf_op jit(solution)/shard_map/ppermute | solution.py:463
  1196.2 65.4 %copy-start.20 = (bf16[512,2048]{1,0:T(8,128)(2,1)S(1)}, bf16[512,2048]{1,0:T(8,128)(2,1)}, u32[]{:S(2)}) copy-start(bf16[512,2048]{1,0:T(8,128)(2,1)} %get-tuple-element.104.x_ref) | copy-start | bytes 6291460
  1268.2 144.7 %collective-permute-start.13 = (f32[1024]{0:T(1024)S(1)}, f32[1024]{0:T(1024)S(1)}, u32[]{:S(2)}, u32[]{:S(2)}) collective-permute-start(f32[1024]{0:T(1024)S(1)} %fusion.81), channel_id=1, source_target_pairs={{0,12},{4,0},{8,4},{12,8},{1,13},{5,1},{9,5},{13,9},{2,14},{6,2},{... | collective-permute-start | bytes 12296 | tf_op jit(solution)/shard_map/ppermute | solution.py:472
  1270.6 142.7 %collective-permute-start.12 = (f32[1024]{0:T(1024)S(1)}, f32[1024]{0:T(1024)S(1)}, u32[]{:S(2)}, u32[]{:S(2)}) collective-permute-start(f32[1024]{0:T(1024)S(1)} %fusion.81), channel_id=1, source_target_pairs={{0,8},{4,12},{8,0},{12,4},{1,9},{5,13},{9,1},{13,5},{2,10},{6,14},... | collective-permute-start | bytes 12296 | tf_op jit(solution)/shard_map/ppermute | solution.py:472
  1287.9 124.4 %collective-permute-start.11 = (f32[1024]{0:T(1024)S(1)}, f32[1024]{0:T(1024)S(1)}, u32[]{:S(2)}, u32[]{:S(2)}) collective-permute-start(f32[1024]{0:T(1024)S(1)} %fusion.81), channel_id=1, source_target_pairs={{0,4},{4,8},{8,12},{12,0},{1,5},{5,9},{9,13},{13,1},{2,6},{6,10},{... | collective-permute-start | bytes 12296 | tf_op jit(solution)/shard_map/ppermute | solution.py:472
  1301.4 283.1 %all-reduce.13.cloned.1.call-start = ((), (), s32[]{:S(2)}) async-start(), calls=%async_computation.8 | async-start | bytes 8388608 | tf_op jit(solution)/shard_map/psum | solution.py:511
  1317.1 121.8 %collective-permute-start.36 = (bf16[1024,1536]{1,0:T(8,128)(2,1)}, bf16[1024,1536]{1,0:T(8,128)(2,1)}, u32[]{:S(2)}, u32[]{:S(2)}) collective-permute-start(bf16[1024,1536]{1,0:T(8,128)(2,1)} %dynamic-slice_bitcast_fusion.2), channel_id=1, source_target_pairs={{0,16},{16,0},{1,17},{17,1},{2,18},{18,2},{3,19},{19,3},{4,20},{20... | collective-permute-start | bytes 9437192 | tf_op jit(solution)/shard_map/ppermute | solution.py:463
  1318.7 65.0 %copy-start.52 = (f32[2048]{0:T(1024)S(1)}, f32[2048]{0:T(1024)}, u32[]{:S(2)}) copy-start(f32[2048]{0:T(1024)} %get-tuple-element.89) | copy-start | bytes 24580
  1412.4 187.3 %collective-permute-start.24 = (f32[4,2048]{1,0:T(4,128)S(1)}, f32[4,2048]{1,0:T(4,128)S(1)}, u32[]{:S(2)}, u32[]{:S(2)}) collective-permute-start(f32[4,2048]{1,0:T(4,128)S(1)} %pad_maximum_fusion.9), channel_id=1, source_target_pairs={{0,16},{16,0},{1,17},{17,1},{2,18},{18,2},{3,19},{19,3},{4,20},{20... | collective-permute-start | bytes 98312 | tf_op jit(solution)/shard_map/ppermute | solution.py:472
  1412.8 143.0 %collective-permute-start.33 = (bf16[704,2048]{1,0:T(8,128)(2,1)}, bf16[704,2048]{1,0:T(8,128)(2,1)}, u32[]{:S(2)}, u32[]{:S(2)}) collective-permute-start(bf16[704,2048]{1,0:T(8,128)(2,1)} %dynamic-slice_bitcast_fusion.5), channel_id=1, source_target_pairs={{0,16},{16,0},{1,17},{17,1},{2,18},{18,2},{3,19},{19,3},{4,20},{20... | collective-permute-start | bytes 8650760 | tf_op jit(solution)/shard_map/ppermute | solution.py:463
  1413.4 148.2 %collective-permute-start.34 = (bf16[1024,2816]{1,0:T(8,128)(2,1)}, bf16[1024,2816]{1,0:T(8,128)(2,1)}, u32[]{:S(2)}, u32[]{:S(2)}) collective-permute-start(bf16[1024,2816]{1,0:T(8,128)(2,1)} %dynamic-slice_bitcast_fusion.1), channel_id=1, source_target_pairs={{0,16},{16,0},{1,17},{17,1},{2,18},{18,2},{3,19},{19,3},{4,20},{20... | collective-permute-start | bytes 17301512 | tf_op jit(solution)/shard_map/ppermute | solution.py:463
  1476.8 290.5 %all-reduce.11.cloned.1.call-start = ((), (), s32[]{:S(2)}) async-start(), calls=%async_computation.7 | async-start | bytes 17301504 | tf_op jit(solution)/shard_map/psum | solution.py:511
  1487.9 63.8 %copy-start.49 = (f32[1,1,2048]{2,1,0:T(1,128)S(1)}, f32[1,1,2048]{2,1,0:T(1,128)}, u32[]{:S(2)}) copy-start(f32[1,1,2048]{2,1,0:T(1,128)} %copy-done.48) | copy-start | bytes 24580
  1487.9 63.8 %copy-start.59 = (f32[512]{0:T(512)S(1)}, f32[512]{0:T(512)}, u32[]{:S(2)}) copy-start(f32[512]{0:T(512)} %add_rsqrt_fusion.2) | copy-start | bytes 6148
  1555.7 48.5 %collective-permute-start.17 = (f32[4,2048]{1,0:T(4,128)S(1)}, f32[4,2048]{1,0:T(4,128)S(1)}, u32[]{:S(2)}, u32[]{:S(2)}) collective-permute-start(f32[4,2048]{1,0:T(4,128)S(1)} %pad_maximum_fusion.8), channel_id=1, source_target_pairs={{0,16},{16,0},{1,17},{17,1},{2,18},{18,2},{3,19},{19,3},{4,20},{20... | collective-permute-start | bytes 98312 | tf_op jit(solution)/shard_map/ppermute | solution.py:472
  1584.5 290.3 %all-reduce.9.cloned.1.call-start = ((), (), s32[]{:S(2)}) async-start(), calls=%async_computation.6 | async-start | bytes 8388608 | tf_op jit(solution)/shard_map/psum | solution.py:511
  1597.1 135.8 %collective-permute-start.32 = (bf16[1024,1536]{1,0:T(8,128)(2,1)}, bf16[1024,1536]{1,0:T(8,128)(2,1)}, u32[]{:S(2)}, u32[]{:S(2)}) collective-permute-start(bf16[1024,1536]{1,0:T(8,128)(2,1)} %dynamic-slice_bitcast_fusion.3), channel_id=1, source_target_pairs={{0,16},{16,0},{1,17},{17,1},{2,18},{18,2},{3,19},{19,3},{4,20},{20... | collective-permute-start | bytes 9437192 | tf_op jit(solution)/shard_map/ppermute | solution.py:463
  1599.7 7.3 collective-permute-start.27
  1603.1 5.1 collective-permute-start.26
  1603.1 6.3 collective-permute-start.25
  1604.2 6.8 collective-permute-start.20
  1607.0 5.4 collective-permute-start.19
  1608.3 5.7 collective-permute-start.18
  1609.4 6.2 collective-permute-start.30
  1611.1 6.2 collective-permute-start.29
  1612.4 7.1 collective-permute-start.28
  1614.0 7.2 collective-permute-start.23
  1615.6 8.2 collective-permute-start.22
  1617.3 25.7 %collective-permute-start.6 = (bf16[256,2048]{1,0:T(8,128)(2,1)S(1)}, bf16[256,2048]{1,0:T(8,128)(2,1)S(1)}, u32[]{:S(2)}, u32[]{:S(2)}) collective-permute-start(bf16[256,2048]{1,0:T(8,128)(2,1)S(1)} %copy-done.44), channel_id=1, source_target_pairs={{0,4},{12,8},{1,5},{13,9},{2,6},{14,10},{3,7},{15,11},{16,20},{28,... | collective-permute-start | bytes 3145736 | tf_op jit(solution)/shard_map/ppermute | solution.py:565
  1619.6 68.4 %collective-permute-start.15 = (f32[256,2048]{1,0:T(8,128)S(1)}, f32[256,2048]{1,0:T(8,128)S(1)}, u32[]{:S(2)}, u32[]{:S(2)}) collective-permute-start(f32[256,2048]{1,0:T(8,128)S(1)} %copy-done.39), channel_id=1, source_target_pairs={{0,4},{12,8},{1,5},{13,9},{2,6},{14,10},{3,7},{15,11},{16,20},{28,... | collective-permute-start | bytes 6291464 | tf_op jit(solution)/shard_map/ppermute | solution.py:565
  1621.2 107.6 %collective-permute-start.14 = (f32[256,2048]{1,0:T(8,128)S(1)}, f32[256,2048]{1,0:T(8,128)}, u32[]{:S(2)}, u32[]{:S(2)}) collective-permute-start(f32[256,2048]{1,0:T(8,128)S(1)} %slice_select_fusion.1), channel_id=1, source_target_pairs={{0,4},{12,8},{1,5},{13,9},{2,6},{14,10},{3,7},{15,11},{16,20},{28,... | collective-permute-start | bytes 6291464 | tf_op jit(solution)/shard_map/ppermute | solution.py:565
  1623.8 5.8 collective-permute-start.21
  1629.6 16.4 collective-permute-start.31
  1630.9 97.9 %copy-start.15 = (f32[512,2048]{1,0:T(8,128)S(1)}, f32[512,2048]{1,0:T(8,128)}, u32[]{:S(2)}) copy-start(f32[512,2048]{1,0:T(8,128)} %get-tuple-element.105) | copy-start | bytes 12582916
  1646.1 131.2 %collective-permute-start.7 = (bf16[256,2048]{1,0:T(8,128)(2,1)}, bf16[256,2048]{1,0:T(8,128)(2,1)S(1)}, u32[]{:S(2)}, u32[]{:S(2)}) collective-permute-start(bf16[256,2048]{1,0:T(8,128)(2,1)} %get-tuple-element.108), channel_id=1, source_target_pairs={{0,16},{16,0},{1,17},{17,1},{2,18},{18,2},{3,19},{19,3},{4,20},{20... | collective-permute-start | bytes 3145736 | tf_op jit(solution)/shard_map/ppermute | solution.py:463
  1732.9 49.2 %collective-permute-start.16 = (f32[256,2048]{1,0:T(8,128)}, f32[256,2048]{1,0:T(8,128)}, u32[]{:S(2)}, u32[]{:S(2)}) collective-permute-start(f32[256,2048]{1,0:T(8,128)} %get-tuple-element.99), channel_id=1, source_target_pairs={{0,16},{16,0},{1,17},{17,1},{2,18},{18,2},{3,19},{19,3},{4,20},{20... | collective-permute-start | bytes 6291464 | tf_op jit(solution)/shard_map/ppermute | solution.py:463
  1771.1 16.2 collective-permute-start.42
  1777.2 112.2 %collective-permute-start.41 = (bf16[1024,2816]{1,0:T(8,128)(2,1)}, bf16[1024,2816]{1,0:T(8,128)(2,1)}, u32[]{:S(2)}, u32[]{:S(2)}) collective-permute-start(bf16[1024,2816]{1,0:T(8,128)(2,1)} %broadcast_select_fusion.2), channel_id=1, source_target_pairs={{0,16},{16,0},{1,17},{17,1},{2,18},{18,2},{3,19},{19,3},{4,20},{20... | collective-permute-start | bytes 17301512 | tf_op jit(solution)/shard_map/ppermute | solution.py:463
  1787.3 87.5 %copy-start.37 = (bf16[256,2048]{1,0:T(8,128)(2,1)S(1)}, bf16[256,2048]{1,0:T(8,128)(2,1)}, u32[]{:S(2)}) copy-start(bf16[256,2048]{1,0:T(8,128)(2,1)} %get-tuple-element.52) | copy-start | bytes 3145732
  1874.9 11.6 collective-permute-start.40
  1886.5 27.7 %collective-permute-start.39 = (bf16[1024,1536]{1,0:T(8,128)(2,1)}, bf16[1024,1536]{1,0:T(8,128)(2,1)}, u32[]{:S(2)}, u32[]{:S(2)}) collective-permute-start(bf16[1024,1536]{1,0:T(8,128)(2,1)} %broadcast_select_fusion.6), channel_id=1, source_target_pairs={{0,16},{16,0},{1,17},{17,1},{2,18},{18,2},{3,19},{19,3},{4,20},{20... | collective-permute-start | bytes 9437192 | tf_op jit(solution)/shard_map/ppermute | solution.py:463
  (77 other events, 788.8 us)
Sparse Core Ops, SparseCore 0:
  10.1 83.4 all-gather.20
  95.8 79.2 all-gather.22
  177.2 23.1 all-gather.12
  202.4 14.8 all-gather.14
  219.2 38.8 all-gather.16
  259.5 24.8 all-gather.18
  1301.5 175.2 all-reduce.14
  1480.8 103.6 all-reduce.12
  1588.8 178.3 all-reduce.10
  1771.2 103.6 all-reduce.8
